TPU v7x, 32 devices: a whole 2x2x4 slice. The times are simulated.
32 devices in a mesh: row: 2 (over y), col: 4 (over z), freq: 4 (over x, core).
Axes of the slice: x: 2, y: 2, z: 4, core: 2. Of those that a mesh axis runs over, the one named last changes fastest.
Arguments:
- signal: bfloat16 [4096, 16896], P(('row', 'col')), may hold values from -6 to 6
- starts: int32 [32], replicated, may hold values from 0 to 15872
- win_len: int32 [32], replicated, may hold values from 512 to 1024, as said below
- chan_factor: bfloat16 [4096, 32], P(('row', 'col')), may hold values from -0.375 to 0.375
- freq_factor: bfloat16 [512, 32], P('freq'), may hold values from -2.1213203 to 2.1213203
Outputs:
- new_chan: float32 [4096, 32], P(('row', 'col'))
- new_freq: float32 [512, 32], P('freq')
Inputs may be any that keep to these rules, and one draw needn't show every extreme that they name: Each segment's window covers its first win_len samples; in every draw some segment's window spans all 1024 samples.
All inputs are finite; a program needn't handle non-finite values.
Results may differ from a plain program's by a relative error of at most 0.0055.
Values may be sent and summed in bfloat16 or wider, within the bound.
No kernel may reach another device: no remote copies, remote signals or barrier semaphores. Data moves between devices by JAX's collectives and lax.ppermute only.
A program may use at most 128 MiB of HBM per device.

v0:
```python
import jax
import jax.numpy as jnp
from jax import lax
from jax.sharding import PartitionSpec as P

NW = 1024
SEGS = 32


def fourier_table(start_bin, bin_count):
    position = jnp.arange(NW, dtype=jnp.int32)[:, None]
    frequency = start_bin + jnp.arange(bin_count, dtype=jnp.int32)[None, :]
    phase = (position * frequency % NW).astype(jnp.float32) * (2.0 * jnp.pi / NW)
    return jnp.stack([jnp.cos(phase), -jnp.sin(phase)], axis=1).astype(jnp.bfloat16)


def taper_table(win_len):
    position = jnp.arange(NW, dtype=jnp.int32)[None, :]
    length = win_len[:, None]
    length_float = length.astype(jnp.float32)
    tapering = 0.5 - 0.5 * jnp.cos(2.0 * jnp.pi * position.astype(jnp.float32) / length_float)
    return jnp.where(position < length, tapering, 0.0) / jnp.sqrt(0.375 * length_float)


def windowed(signal, starts, win_len):
    indices = starts[:, None] + jnp.arange(NW, dtype=jnp.int32)[None, :]
    portions = jnp.take(signal, indices, axis=1)
    return (portions.astype(jnp.float32) * taper_table(win_len)[None]).astype(jnp.bfloat16)


def solve_gram(system, contracted):
    factor_low = jnp.linalg.cholesky(system)
    middle = lax.linalg.triangular_solve(
        factor_low, contracted, left_side=False, lower=True, transpose_a=True
    )
    return lax.linalg.triangular_solve(
        factor_low, middle, left_side=False, lower=True, transpose_a=False
    )


def body(signal, starts, win_len, chan_factor, freq_factor):
    local_chan = signal.shape[0]
    local_bins = freq_factor.shape[0]
    start_bin = lax.axis_index("freq") * local_bins
    transform = fourier_table(start_bin, local_bins).reshape(NW, 2 * local_bins)
    segments = windowed(signal, starts, win_len)
    product = jnp.dot(
        segments.reshape(local_chan * SEGS, NW), transform, preferred_element_type=jnp.float32
    )
    spectra = product.astype(jnp.bfloat16).reshape(local_chan, SEGS, 2, local_bins)
    gram_w_part = jnp.dot(freq_factor.T, freq_factor, preferred_element_type=jnp.float32)
    weight_rows = freq_factor.T.astype(jnp.float32)
    gram_b_part = jnp.dot(chan_factor.T, chan_factor, preferred_element_type=jnp.float32)
    summed_part = jnp.einsum(
        "ckzf,cr->kzrf", spectra, chan_factor, preferred_element_type=jnp.float32
    )
    summed, gram_b = lax.psum((summed_part, gram_b_part), ("row", "col"))
    weighted = (summed * weight_rows[None, None] / SEGS).astype(jnp.bfloat16)
    contracted_part = jnp.einsum(
        "ckzf,kzrf->cr", spectra, weighted, preferred_element_type=jnp.float32
    )
    contracted, gram_w = lax.psum((contracted_part, gram_w_part), "freq")
    new_chan = solve_gram(gram_b * gram_w, contracted)
    rounded = new_chan.astype(jnp.bfloat16)
    gram_a_part = jnp.dot(new_chan.T, new_chan, precision=lax.Precision.HIGHEST)
    images_part = jnp.einsum("ckzf,cr->kzrf", spectra, rounded, preferred_element_type=jnp.float32)
    images, gram_a = lax.psum((images_part, gram_a_part), ("row", "col"))
    freq_terms = jnp.einsum("kzrf,kzrf->fr", images, summed, precision=lax.Precision.HIGHEST) / SEGS
    new_freq = solve_gram(gram_a * gram_b, freq_terms)
    return (new_chan, new_freq)


def solution(mesh):
    return jax.shard_map(
        body,
        mesh=mesh,
        in_specs=(P(("row", "col"), None), P(), P(), P(("row", "col"), None), P("freq", None)),
        out_specs=(P(("row", "col"), None), P("freq", None)),
        check_vma=False,
    )
```

profile of v0, /device:TPU:0, one launch (start us, length us, event | category | flops | bytes accessed | tf_op | source)
XLA Modules:
  0.0 508.4 jit_solution(8843169777012017422)
XLA Ops:
  7.2 0.7 multiply_sqrt_fusion
  7.9 0.7 convert_element_type.78
  8.6 0.7 fusion.27
  9.3 0.8 fusion.30
  10.1 22.7 %copy.32 = bf16[512,16896]{0,1:T(8,128)(2,1)} copy(bf16[512,16896]{1,0:T(8,128)(2,1)} %param.6) | data formatting | bytes 34603008 | tf_op args[0]
  32.8 140.2 %gather_fusion = bf16[32768,512]{1,0:T(8,128)(2,1)} fusion(bf16[512,16896]{0,1:T(8,128)(2,1)} %copy.32, s32[32768]{0:T(1024)S(1)} %broadcast_clamp_fusion), kind=kCustom, calls=%fused_computation | custom fusion | bytes 67239936 | tf_op jit(solution)/shard_map/jit(_take)/gather | solution.py:27
  173.0 46.7 %copy.33 = bf16[32,1024,512]{1,0,2:T(8,128)(2,1)} copy(bf16[32,1024,512]{2,1,0:T(8,128)(2,1)} %bitcast.66) | data formatting | bytes 67108864 | tf_op jit(solution)/shard_map/jit(_take)/gather | solution.py:27
  219.7 2.2 cosine_convert_fusion
  222.2 0.5 fusion.26
  222.7 23.4 %multiply_convert_fusion = bf16[32,1024,512]{1,0,2:T(8,128)(2,1)} fusion(f32[32,1024]{1,0:T(8,128)S(1)} %fusion.26, bf16[32,1024,512]{1,0,2:T(8,128)(2,1)} %copy.33, pred[32,1024]{1,0:T(8,128)(4,1)S(1)} %fusion.30), kind=kLoop, calls=%fused_computation.1 | loop fusion | flops 67108864 | bytes 67272704 | tf_op jit(solution)/shard_map/convert_element_type | solution.py:28
  246.1 17.1 %convolution_convert_fusion = bf16[16384,256]{1,0:T(8,128)(2,1)} fusion(bf16[16384,1024]{1,0:T(8,128)(2,1)} %bitcast.67, bf16[1024,256]{0,1:T(8,128)(2,1)S(1)} %bitcast.68), kind=kOutput, calls=%fused_computation.2 | convolution fusion | flops 8594128896 | bytes 42467328 | tf_op jit(solution)/shard_map/dot_general | solution.py:47
  263.2 12.6 %reshape.276 = bf16[512,32,2,128]{3,2,1,0:T(2,128)(2,1)} reshape(bf16[16384,256]{1,0:T(8,128)(2,1)} %convolution_convert_fusion) | data formatting | bytes 16777216 | tf_op jit(solution)/shard_map/reshape | solution.py:50
  275.8 9.2 %fusion.6 = f32[32,2,32,128]{3,2,1,0:T(8,128)} fusion(bf16[512,32,2,128]{3,2,1,0:T(2,128)(2,1)} %reshape.276, bf16[512,32]{0,1:T(8,128)(2,1)S(1)} %copy-done), kind=kOutput, calls=%fused_computation.9 | convolution fusion | flops 268435456 | bytes 9469952 | tf_op jit(solution)/shard_map/ckzf,cr->kzrf/dot_general | solution.py:54
  285.1 39.7 %psum.44 = f32[32,32]{0,1:T(8,128)S(1)} all-reduce(f32[32,32]{0,1:T(8,128)S(1)} %fusion.50), channel_id=1, replica_groups=mesh['row'=2,'col'=4,'freq'=4] {'row','col'}, use_global_device_ids=true, to_apply=%region_2.3 | all-reduce | flops 1024 | bytes 8192 | tf_op jit(solution)/shard_map/psum | solution.py:57
  324.9 10.1 %psum.45 = f32[32,32]{0,1:T(8,128)S(1)} all-reduce(f32[32,32]{0,1:T(8,128)S(1)} %fusion.51), channel_id=1, replica_groups=mesh['row'=2,'col'=4,'freq'=4] {'freq'}, use_global_device_ids=true, to_apply=%region_3.4 | all-reduce | flops 1024 | bytes 8192 | tf_op jit(solution)/shard_map/psum | solution.py:62
  335.1 2.9 cholesky.44
  338.1 0.6 compare_reduce_fusion.1
  338.7 28.0 %all-reduce.4.cloned.1.call-done = f32[32,2,32,128]{3,2,1,0:T(8,128)} async-done(((f32[32,2,32,128]{3,2,1,0:T(8,128)}), f32[32,2,32,128]{3,2,1,0:T(8,128)}) %all-reduce.4.cloned.1.call-update) | async-done | bytes 1048592 | tf_op jit(solution)/shard_map/psum | solution.py:57
  366.7 12.8 %fusion.12 = f32[512,32]{0,1:T(8,128)} fusion(bf16[512,32,2,128]{3,2,1,0:T(2,128)(2,1)} %reshape.276, f32[32,2,32,128]{3,2,1,0:T(8,128)} %all-reduce.4.cloned.1.call-done, f32[32,128]{1,0:T(8,128)S(1)} %convert_bitcast_fusion), kind=kOutput, calls=%fused_computation.11 | convolution fusion | flops 269221888 | bytes 9519104 | tf_op jit(solution)/shard_map/ckzf,kzrf->cr/dot_general | solution.py:59
  379.8 0.7 fusion.37
  380.4 2.4 custom-call.12
  382.9 27.4 %all-reduce.6.cloned.1.call-done = f32[512,32]{0,1:T(8,128)} async-done(((f32[512,32]{0,1:T(8,128)}), f32[512,32]{0,1:T(8,128)}) %all-reduce.6.cloned.1.call-update) | async-done | bytes 65552 | tf_op jit(solution)/shard_map/psum | solution.py:62
  410.3 1.1 fusion.45
  411.6 9.1 %fusion.9 = f32[32,2,32,128]{3,2,1,0:T(8,128)} fusion(bf16[512,32,2,128]{3,2,1,0:T(2,128)(2,1)} %reshape.276, f32[512,32]{0,1:T(8,128)S(1)} %fusion.43), kind=kOutput, calls=%fused_computation.10 | convolution fusion | flops 268451840 | bytes 9502720 | tf_op jit(solution)/shard_map/ckzf,cr->kzrf/dot_general | solution.py:66
  421.0 37.7 %psum.47 = f32[32,32]{0,1:T(8,128)S(1)} all-reduce(f32[32,32]{0,1:T(8,128)S(1)} %fusion.52), channel_id=1, replica_groups=mesh['row'=2,'col'=4,'freq'=4] {'row','col'}, use_global_device_ids=true, to_apply=%region_7.9 | all-reduce | flops 1024 | bytes 8192 | tf_op jit(solution)/shard_map/psum | solution.py:67
  458.8 2.9 cholesky.55
  461.8 0.6 compare_reduce_fusion
  462.4 0.7 fusion.38
  463.1 2.4 custom-call.13
  465.5 33.9 %all-reduce.8.cloned.1.call-done = f32[32,2,32,128]{3,2,1,0:T(8,128)} async-done(((f32[32,2,32,128]{3,2,1,0:T(8,128)}), f32[32,2,32,128]{3,2,1,0:T(8,128)}) %all-reduce.8.cloned.1.call-update) | async-done | bytes 1048592 | tf_op jit(solution)/shard_map/psum | solution.py:67
  499.4 1.4 multiply_reduce_fusion
  501.1 0.8 fusion.39
  (37 shorter events, 1.9 us)
Async XLA Ops:
  7.2 268.6 %copy-start = (bf16[512,32]{0,1:T(8,128)(2,1)S(1)}, bf16[512,32]{0,1:T(8,128)(2,1)}, u32[]{:S(2)}) copy-start(bf16[512,32]{0,1:T(8,128)(2,1)} %param.9) | copy-start | bytes 98308
  7.2 359.5 %all-reduce.4.cloned.1.call-start = ((), (), s32[]{:S(2)}) async-start(), calls=%async_computation | async-start | bytes 2097152 | tf_op jit(solution)/shard_map/psum | solution.py:57
  173.0 49.2 %copy-start.4 = (s32[32]{0:T(128)S(1)}, s32[32]{0:T(128)}, u32[]{:S(2)}) copy-start(s32[32]{0:T(128)} %param.8) | copy-start | bytes 388
  263.2 61.6 %copy-start.3 = (bf16[128,32]{0,1:T(8,128)(2,1)S(1)}, bf16[128,32]{0,1:T(8,128)(2,1)}, u32[]{:S(2)}) copy-start(bf16[128,32]{0,1:T(8,128)(2,1)} %param.10) | copy-start | bytes 24580
  284.9 125.4 %all-reduce.6.cloned.1.call-start = ((), (), s32[]{:S(2)}) async-start(), calls=%async_computation.1 | async-start | bytes 131072 | tf_op jit(solution)/shard_map/psum | solution.py:62
  366.7 132.7 %copy-start.2 = (f32[32,2,32,128]{3,2,1,0:T(8,128)S(1)}, f32[32,2,32,128]{3,2,1,0:T(8,128)}, u32[]{:S(2)}) copy-start(f32[32,2,32,128]{3,2,1,0:T(8,128)} %all-reduce.4.cloned.1.call-done) | copy-start | bytes 3145732
  379.5 119.9 %all-reduce.8.cloned.1.call-start = ((), (), s32[]{:S(2)}) async-start(), calls=%async_computation.2 | async-start | bytes 2097152 | tf_op jit(solution)/shard_map/psum | solution.py:67
  411.6 90.3 %copy-start.1 = (f32[512,32]{0,1:T(8,128)}, f32[512,32]{0,1:T(8,128)S(1)}, u32[]{:S(2)}) copy-start(f32[512,32]{0,1:T(8,128)S(1)} %fusion.43) | copy-start | bytes 196612
Sparse Core Ops, SparseCore 0:
  285.1 81.5 all-reduce.3
  379.6 30.6 all-reduce.5
  420.9 78.4 all-reduce.7
where the time goes:
time: 511 us; the launch traced here: 508 us
  local copies, waits for them, and re-layouts  223 us (44%)
  waiting for transfers between devices  89.4 us (17%)
  blocking collectives  87.6 us (17%)
  matrix products  50.9 us (10%)
  other arithmetic  43.8 us (9%)
  between operations  13.9 us (3%)
    gather x2, local copies, waits for them, and re-layouts, windowed(): portions = jnp.take(signal, indices, axis=1)  187 us
    psum x1, blocking collectives, body(): summed, gram_b = lax.psum((summed_part, gram_b_part), ('row', 'col'))  39.7 us
    psum x1, blocking collectives, body(): images, gram_a = lax.psum((images_part, gram_a_part), ('row', 'col'))  37.7 us
    psum x1, waiting for transfers between devices, body(): images, gram_a = lax.psum((images_part, gram_a_part), ('row', 'col'))  33.9 us
    psum x1, waiting for transfers between devices, body(): summed, gram_b = lax.psum((summed_part, gram_b_part), ('row', 'col'))  28 us
    psum x1, waiting for transfers between devices, body(): contracted, gram_w = lax.psum((contracted_part, gram_w_part), 'freq')  27.4 us
    convert_element_type x1, other arithmetic, windowed(): (portions.astype(jnp.float32) * taper_table(win_len)[None]).astype(jnp.bf...  23.4 us
    unnamed x12, local copies, waits for them, and re-layouts  22.7 us
  transfers between devices with their start and end apart: 3, of which 3 were waited for; matrix products, arithmetic and copies ran while one was open for 3% of the time, Pallas kernels for 0%

commit v1 on v0

v1 whole, which is shorter than its diff:
```python
import jax
import jax.numpy as jnp
import numpy as np
from jax import lax
from jax.experimental import pallas as pl
from jax.experimental.pallas import tpu as pltpu
from jax.sharding import PartitionSpec as P

NW = 1024
HALF = NW // 2
SEGS = 32
LANES = 128
ALL = ("row", "col", "freq")
F32 = jnp.float32
BF16 = jnp.bfloat16
HIGHEST = lax.Precision.HIGHEST
VMEM_BYTES = 48 << 20


def half_table():
    position = np.arange(HALF)
    phase = (np.outer(position, position) % NW) * (2.0 * np.pi / NW)
    table = np.concatenate([np.cos(phase), -np.sin(phase)], axis=1)
    return jnp.asarray(table.astype(np.float32)).astype(BF16)


def iota(shape, axis):
    return lax.broadcasted_iota(jnp.int32, shape, axis)


def dot(a, b, contract=((1,), (0,)), precision=None):
    return lax.dot_general(
        a, b, (contract, ((), ())), precision=precision, preferred_element_type=F32
    )


def spd_inverse(system):
    size = system.shape[0]
    rows, cols = iota((size, size), 0), iota((size, size), 1)
    for i in range(size):
        row, col = system[i : i + 1, :], system[:, i : i + 1]
        pivot = 1.0 / system[i : i + 1, i : i + 1]
        scaled = row * pivot
        here, there = rows == i, cols == i
        updated = system - col * scaled
        updated = jnp.where(there, col * pivot, updated)
        updated = jnp.where(here, scaled, updated)
        system = jnp.where(here & there, -pivot, updated)
    return -system


def split_rows(gram, size):
    spread = (iota((size, LANES), 1) % size == iota((size, LANES), 0)).astype(F32)
    tiled = dot(gram, spread, precision=HIGHEST)
    high = tiled.astype(BF16).astype(F32)
    return jnp.where(iota((size, LANES), 1) // size % 2 == 0, high, tiled - high)


def join_rows(ref, group):
    value = ref[...]
    value = value + pltpu.roll(value, LANES - 32, 1)
    other = pltpu.roll(value, 64, 1)
    return jnp.where(iota(value.shape, 0) % group < group // 2, value, other)[:, :32]


def packed_side(ref, start, count):
    upper = ref[pl.ds(start, count), :]
    lower = ref[pl.ds(start + count, count), :]
    return jnp.where(iota((count, LANES), 1) < 64, upper, lower)


def taper_of(win_ref):
    length = jnp.zeros((SEGS, LANES), F32)
    which = iota((SEGS, LANES), 0)
    for k in range(SEGS):
        length = jnp.where(which == k, win_ref[k].astype(F32), length)
    norm = 1.0 / (0.375 * length)
    scale = jnp.sqrt(norm)
    pieces = []
    for j in range(NW // LANES):
        position = (iota((SEGS, LANES), 1) + j * LANES).astype(F32)
        angle = jnp.pi * (position / length - 0.5)
        square = angle * angle
        value = 1.0 + square * (
            -1.0 / 2
            + square
            * (
                1.0 / 24
                + square
                * (
                    -1.0 / 720
                    + square
                    * (1.0 / 40320 + square * (-1.0 / 3628800 + square * (1.0 / 479001600)))
                )
            )
        )
        pieces.append(jnp.where(position < length, value * value * scale, 0.0))
    return jnp.concatenate(pieces, axis=1)


def windows(z_ref, y_ref, starts_ref):
    lane = iota((8, LANES), 1)
    for k in range(SEGS):
        start = starts_ref[k]
        major, minor = start // LANES, start % LANES
        mixed = jnp.where(lane >= minor, z_ref[pl.ds(major, 8), :], z_ref[pl.ds(major + 1, 8), :])
        y_ref[k] = pltpu.roll(mixed, (LANES - minor) % LANES, 1)
    return jnp.concatenate([y_ref[:, j, :] for j in range(8)], axis=1)


def forward(samples, table):
    low, high = samples[:, :HALF], samples[:, HALF:]
    both = jnp.concatenate([low + high, low - high], axis=0)
    top = both.astype(BF16)
    rest = (both - top.astype(F32)).astype(BF16)
    out = dot(jnp.concatenate([top, rest], axis=0), table)
    out = out[: 2 * SEGS] + out[2 * SEGS :]
    return jnp.where(iota((SEGS, NW), 1) % 2 == 0, out[:SEGS], out[SEGS:])


def body(signal, starts, win_len, chan_factor, freq_factor):
    mesh_size = {name: lax.axis_size(name) for name in ALL}
    nq = mesh_size["freq"]
    nc = mesh_size["row"] * mesh_size["col"]
    ndev = nq * nc
    chans, samples = signal.shape
    bins, rank = freq_factor.shape
    span = samples // nq
    rows = span // LANES
    total_rows = rows * nq
    freq_row, b_row, w_row = rows, rows + 1, rows + 5
    msg_rows = rows + 7
    chunks = 3
    chunk = span // chunks
    assert rank == 32 and nq == 4 and bins == LANES and ndev >= rank and nc % 8 == 0
    assert span % (chunks * LANES) == 0 and msg_rows % 8 == 0

    vmem = pl.BlockSpec(memory_space=pltpu.VMEM)
    smem = pl.BlockSpec(memory_space=pltpu.SMEM)
    hbm = pl.BlockSpec(memory_space=pl.ANY)
    params = pltpu.CompilerParams(vmem_limit_bytes=VMEM_BYTES)
    table = half_table()
    msg = jax.ShapeDtypeStruct((ndev, msg_rows, LANES), BF16)

    def fetch(signal_ref, buf, sem):
        base = lax.axis_index("freq") * span
        copies = []
        for i in range(chunks):
            where = pl.multiple_of(base + i * chunk, LANES)
            copies.append(
                pltpu.make_async_copy(
                    signal_ref.at[:, pl.ds(where, chunk)], buf.at[i], sem.at[i]
                )
            )
        for copy in copies:
            copy.start()
        return copies

    signal_scratch = [
        pltpu.VMEM((chunks, chans, chunk), BF16),
        pltpu.SemaphoreType.DMA((chunks,)),
    ]

    def channel_sums(lhs, copies, buf, out_ref):
        if ndev > rank:
            out_ref[...] = jnp.zeros_like(out_ref)
        for i in range(chunks):
            copies[i].wait()
            part = dot(lhs, buf[i])
            for j in range(chunk // LANES):
                out_ref[:rank, i * (chunk // LANES) + j, :] = part[:, j * LANES : (j + 1) * LANES]

    def sums_kernel(signal_ref, win_ref, chan_ref, freq_ref, msg_ref, taper_ref, buf, sem, out, gs):
        copies = fetch(signal_ref, buf, sem)
        q = lax.axis_index("freq")
        c = lax.axis_index("row") * mesh_size["col"] + lax.axis_index("col")
        taper_ref[...] = taper_of(win_ref)
        chan = chan_ref[...].astype(F32).T
        chan_low = chan.astype(BF16)
        weights = freq_ref[...].astype(F32).T
        channel_sums(chan_low, copies, buf, out)
        out[:rank, freq_row, :] = weights
        gs[...] = split_rows(dot(chan_low, chan_low, ((1,), (1,))), rank)
        side = packed_side(gs, q * 8, 4)
        out[:, b_row : b_row + 4, :] = jnp.broadcast_to(side[None], (ndev, 4, LANES))
        weights_low = weights.astype(BF16)
        gs[...] = split_rows(dot(weights_low, weights_low, ((1,), (1,))), rank)
        side = packed_side(gs, (c % 8) * 4, 2)
        out[:, w_row : w_row + 2, :] = jnp.broadcast_to(side[None], (ndev, 2, LANES))
        msg_ref[...] = out[...].astype(BF16)

    message, taper = pl.pallas_call(
        sums_kernel,
        out_shape=(msg, jax.ShapeDtypeStruct((SEGS, NW), F32)),
        in_specs=[hbm, smem, vmem, vmem],
        out_specs=(vmem, vmem),
        scratch_shapes=signal_scratch
        + [pltpu.VMEM((ndev, msg_rows, LANES), F32), pltpu.VMEM((rank, LANES), F32)],
        compiler_params=params,
        name="channel_sums",
    )(signal, win_len, chan_factor, freq_factor)
    received = lax.all_to_all(message, ALL, 0, 0, tiled=True)

    z_rows = (total_rows + 8 + 7) // 8 * 8

    def gather_rank(rcv_ref, z_ref, gs):
        for q in range(nq):
            total = rcv_ref[q].astype(F32)
            for c in range(1, nc):
                total = total + rcv_ref[c * nq + q].astype(F32)
            z_ref[q * rows : (q + 1) * rows, :] = total[:rows]
            gs[8 * q : 8 * q + 4, :] = total[b_row : b_row + 4]
            gs[8 * q + 4 : 8 * q + 8, :] = total[b_row : b_row + 4]
        z_ref[total_rows:, :] = jnp.zeros((z_rows - total_rows, LANES), F32)
        return join_rows(gs, 8)

    def weight_kernel(
        rcv_ref, starts_ref, taper_ref, table_ref,
        msg_ref, summed_ref, inverse_ref, gram_ref,
        z_ref, y_ref, gs, u_ref,
    ):
        gram_b = gather_rank(rcv_ref, z_ref, gs)
        gram_ref[...] = gram_b
        for c in range(8):
            side = rcv_ref[c * nq].astype(F32)[w_row : w_row + 2]
            for q in range(1, nq):
                side = side + rcv_ref[c * nq + q].astype(F32)[w_row : w_row + 2]
            gs[4 * c : 4 * c + 2, :] = side
            gs[4 * c + 2 : 4 * c + 4, :] = side
        gram_w = join_rows(gs, 4)
        inverse_ref[...] = spd_inverse(gram_b * gram_w)
        taper = taper_ref[...]
        table = table_ref[...]
        summed = forward(windows(z_ref, y_ref, starts_ref) * taper, table)
        summed_ref[...] = summed
        weight = jnp.concatenate(
            [rcv_ref[q].astype(F32)[freq_row : freq_row + 1] for q in range(nq)] * 2, axis=1
        )
        weighted = summed * weight / SEGS
        even = iota((SEGS, NW), 1) % 2 == 0
        masked = jnp.concatenate(
            [jnp.where(even, weighted, 0.0), jnp.where(even, 0.0, weighted)], axis=0
        ).astype(BF16)
        back = dot(masked[:, :HALF], table[:, :HALF]) + dot(masked[:, HALF:], table[:, HALF:])
        back = jnp.concatenate(
            [back[:SEGS] + back[SEGS:], back[:SEGS] - back[SEGS:]], axis=1
        )
        back = back * taper
        for j in range(8):
            y_ref[:, j, :] = back[:, j * LANES : (j + 1) * LANES]
        u_ref[...] = jnp.zeros_like(u_ref)
        lane = iota((8, LANES), 1)
        for k in range(SEGS):
            start = starts_ref[k]
            major, minor = start // LANES, start % LANES
            turned = pltpu.roll(y_ref[k], minor, 1)
            first = pl.ds(major, 8)
            u_ref[k % 2, first, :] += jnp.where(lane >= minor, turned, 0.0)
            second = pl.ds(major + 1, 8)
            u_ref[k % 2, second, :] += jnp.where(lane < minor, turned, 0.0)
        added = u_ref[0] + u_ref[1]
        pad = jnp.zeros((msg_rows - rows, LANES), F32)
        for q in range(nq):
            piece = jnp.concatenate([added[q * rows : (q + 1) * rows], pad], axis=0).astype(BF16)
            for c in range(nc):
                msg_ref[c * nq + q] = piece

    square = jax.ShapeDtypeStruct((rank, rank), F32)
    message, summed, inverse, gram_b = pl.pallas_call(
        weight_kernel,
        out_shape=(msg, jax.ShapeDtypeStruct((SEGS, NW), F32), square, square),
        in_specs=[vmem, smem, vmem, vmem],
        out_specs=(vmem,) * 4,
        scratch_shapes=[
            pltpu.VMEM((z_rows, LANES), F32),
            pltpu.VMEM((SEGS, 8, LANES), F32),
            pltpu.VMEM((rank, LANES), F32),
            pltpu.VMEM((2, z_rows, LANES), F32),
        ],
        compiler_params=params,
        name="weighting",
    )(received, starts, taper, table)
    received = lax.all_to_all(message, ALL, 0, 0, tiled=True)

    def contract_kernel(signal_ref, rcv_ref, inverse_ref, part_ref, buf, sem, out):
        copies = fetch(signal_ref, buf, sem)
        out[...] = rcv_ref[:rank].astype(F32)
        total = jnp.zeros((rank, chans), F32)
        for i in range(chunks):
            pieces = [out[:, i * (chunk // LANES) + j, :] for j in range(chunk // LANES)]
            operand = jnp.concatenate(pieces, axis=1).astype(BF16)
            copies[i].wait()
            total = total + dot(operand, buf[i], ((1,), (1,)))
        part_ref[...] = dot(inverse_ref[...], total, precision=HIGHEST).astype(BF16)

    part = pl.pallas_call(
        contract_kernel,
        out_shape=jax.ShapeDtypeStruct((rank, chans), BF16),
        in_specs=[hbm, vmem, vmem],
        out_specs=vmem,
        scratch_shapes=signal_scratch + [pltpu.VMEM((rank, msg_rows, LANES), F32)],
        compiler_params=params,
        name="contraction",
    )(signal, received, inverse)
    parts = [part] + [
        lax.ppermute(part, "freq", [(i, i ^ m) for i in range(nq)]) for m in range(1, nq)
    ]

    def images_kernel(signal_ref, p0, p1, p2, p3, chan_ref, msg_ref, buf, sem, out, gs):
        copies = fetch(signal_ref, buf, sem)
        q = lax.axis_index("freq")
        pair = p0[...].astype(F32) + p1[...].astype(F32)
        new_chan = pair + (p2[...].astype(F32) + p3[...].astype(F32))
        chan_ref[...] = new_chan.T
        channel_sums(new_chan.astype(BF16), copies, buf, out)
        gs[...] = split_rows(dot(new_chan, new_chan, ((1,), (1,)), HIGHEST), rank)
        side = packed_side(gs, q * 8, 4)
        out[:, freq_row:, :] = jnp.zeros((ndev, msg_rows - rows, LANES), F32)
        out[:, b_row : b_row + 4, :] = jnp.broadcast_to(side[None], (ndev, 4, LANES))
        msg_ref[...] = out[...].astype(BF16)

    new_chan, message = pl.pallas_call(
        images_kernel,
        out_shape=(jax.ShapeDtypeStruct((chans, rank), F32), msg),
        in_specs=[hbm] + [vmem] * 4,
        out_specs=(vmem, vmem),
        scratch_shapes=signal_scratch
        + [pltpu.VMEM((ndev, msg_rows, LANES), F32), pltpu.VMEM((rank, LANES), F32)],
        compiler_params=params,
        name="image_sums",
    )(signal, *parts)
    received = lax.all_to_all(message, ALL, 0, 0, tiled=True)

    def terms_kernel(
        rcv_ref, starts_ref, taper_ref, table_ref, summed_ref, gram_ref,
        terms_ref, inverse_ref, z_ref, y_ref, gs,
    ):
        gram_a = gather_rank(rcv_ref, z_ref, gs)
        inverse_ref[...] = spd_inverse(gram_a * gram_ref[...])
        images = forward(windows(z_ref, y_ref, starts_ref) * taper_ref[...], table_ref[...])
        terms = jnp.sum(images * summed_ref[...], axis=0, keepdims=True) / SEGS
        terms = terms[:, :HALF] + terms[:, HALF:]
        for d in range(ndev):
            q = d % nq
            terms_ref[d] = terms[:, q * bins : (q + 1) * bins]

    terms, inverse = pl.pallas_call(
        terms_kernel,
        out_shape=(jax.ShapeDtypeStruct((ndev, 1, bins), F32), square),
        in_specs=[vmem, smem, vmem, vmem, vmem, vmem],
        out_specs=(vmem, vmem),
        scratch_shapes=[
            pltpu.VMEM((z_rows, LANES), F32),
            pltpu.VMEM((SEGS, 8, LANES), F32),
            pltpu.VMEM((rank, LANES), F32),
        ],
        compiler_params=params,
        name="frequency_terms",
    )(received, starts, taper, table, summed, gram_b)
    terms = lax.all_to_all(terms, ALL, 0, 0, tiled=True)

    def finish_kernel(terms_ref, inverse_ref, out_ref):
        gathered = terms_ref[:rank, 0, :]
        out_ref[...] = dot(gathered, inverse_ref[...], ((0,), (0,)), HIGHEST)

    new_freq = pl.pallas_call(
        finish_kernel,
        out_shape=jax.ShapeDtypeStruct((bins, rank), F32),
        in_specs=[vmem, vmem],
        out_specs=vmem,
        compiler_params=params,
        name="frequency_solve",
    )(terms, inverse)
    return (new_chan, new_freq)


def solution(mesh):
    return jax.shard_map(
        body,
        mesh=mesh,
        in_specs=(P(("row", "col"), None), P(), P(), P(("row", "col"), None), P("freq", None)),
        out_specs=(P(("row", "col"), None), P("freq", None)),
        check_vma=False,
    )
```

time: 511 us -> 85.2 us (0.17)
  local copies, waits for them, and re-layouts: 223 us -> 3.86 us
  waiting for transfers between devices: 89.4 us -> 9.12 us
  matrix products: 50.9 us -> 0 us
  other arithmetic: 43.8 us -> 0 us
  blocking collectives: 87.6 us -> 46.5 us
  Pallas kernels: 0 us -> 20.3 us
  between operations: 13.9 us -> 0.71 us
    gather x2 -> x0, local copies, waits for them, and re-layouts: 187 us -> none  [windowed(): portions = jnp.take(signal, indices, axis=1)]
    psum x3 -> x0, waiting for transfers between devices: 89.3 us -> none  [the longest x1 33.9 us: body(): images, gram_a = lax.psum((images_part, gram_a_part), ('row', 'col'))]
    psum x3 -> x0, blocking collectives: 87.6 us -> none  [the longest x1 39.7 us: body(): summed, gram_b = lax.psum((summed_part, gram_b_part), ('row', 'col'))]
    dot_general x7 -> x0, matrix products: 48.6 us -> none  [the longest x1 17.1 us: body(): jnp.dot(segments.reshape(local_chan * SEGS, NW), transform, preferred_ele...]
    all_to_all x0 -> x3, blocking collectives: none -> 46.5 us  [body(): received = lax.all_to_all(message, ALL, 0, 0, tiled=True)]
    convert_element_type x3 -> x0, other arithmetic: 24.1 us -> none  [the longest x1 23.4 us: windowed(): (portions.astype(jnp.float32) * taper_table(win_len)[None]).astype(jnp.bf...]
    pallas_call x0 -> x6, Pallas kernels: none -> 20.3 us  [the longest x1 5.19 us: body(): pl.pallas_call(terms_kernel, out_shape=(jax.ShapeDtypeStruct((ndev, 1, bi...]
    unnamed x12 -> x10, local copies, waits for them, and re-layouts: 22.7 us -> 3.86 us
  transfers between devices with their start and end apart: 3 -> 4, of which waited for: 3 -> 3; matrix products, arithmetic and copies ran while one was open for 3% -> 1% of each run, Pallas kernels for 0% -> 0%
where the time goes in v1:
time: 85.2 us; the launch traced here: 84.9 us
  blocking collectives  46.5 us (55%)
  Pallas kernels  20.3 us (24%)
  waiting for transfers between devices  9.12 us (11%)
  starting transfers between devices  4.47 us (5%)
  local copies, waits for them, and re-layouts  3.86 us (5%)
    all_to_all x3, blocking collectives, body(): received = lax.all_to_all(message, ALL, 0, 0, tiled=True)  46.5 us
    all_to_all x1, waiting for transfers between devices, body(): terms = lax.all_to_all(terms, ALL, 0, 0, tiled=True)  6.33 us
    pallas_call x1, Pallas kernels, body(): pl.pallas_call(terms_kernel, out_shape=(jax.ShapeDtypeStruct((ndev, 1, bi...  5.19 us
    pallas_call x1, Pallas kernels, body(): pl.pallas_call(weight_kernel, out_shape=(msg, jax.ShapeDtypeStruct((SEGS,...  5.02 us
    unnamed x10, local copies, waits for them, and re-layouts  3.86 us
    pallas_call x1, Pallas kernels, body(): pl.pallas_call(sums_kernel, out_shape=(msg, jax.ShapeDtypeStruct((SEGS, N...  3.44 us
    pallas_call x1, Pallas kernels, body(): pl.pallas_call(contract_kernel, out_shape=jax.ShapeDtypeStruct((rank, cha...  3.44 us
    pallas_call x1, Pallas kernels, body(): pl.pallas_call(images_kernel, out_shape=(jax.ShapeDtypeStruct((chans, ran...  2.92 us
  transfers between devices with their start and end apart: 4, of which 3 were waited for; matrix products, arithmetic and copies ran while one was open for 1% of the time, Pallas kernels for 0%

profile of v1, /device:TPU:0, one launch (start us, length us, event | category | flops | bytes accessed | tf_op | source)
XLA Modules:
  0.0 84.9 jit_solution(4833316376124535575)
XLA Ops:
  0.6 0.0 copy-start
  0.6 0.0 copy-start.1
  0.7 0.9 %copy.9.freq_ref = bf16[128,32]{1,0:T(8,128)(2,1)S(1)} copy(bf16[128,32]{0,1:T(8,128)(2,1)} %param.10) | data formatting | bytes 16384 | tf_op args[4]
  1.5 0.9 %copy.8.chan_ref = bf16[512,32]{1,0:T(8,128)(2,1)S(1)} copy(bf16[512,32]{0,1:T(8,128)(2,1)} %param.9) | data formatting | bytes 65536 | tf_op args[3]
  2.4 0.0 copy-start.2
  2.4 0.6 copy-done.2
  3.1 3.4 %channel_sums.1 = (bf16[32,40,128]{2,1,0:T(8,128)(2,1)S(1)}, f32[32,1024]{1,0:T(8,128)S(1)}) custom-call(bf16[512,16896]{1,0:T(8,128)(2,1)} %signal_ref.5, s32[32]{0:T(128)S(1)} %copy-done.2, bf16[512,32]{1,0:T(8,128)(2,1)S(1)} %copy.8.chan_ref, bf16[128,32]{1,0:T(8,128)(2,1)S(1)} %copy.9.freq_ref), custom_call_target="tpu_custom_call" | custom-call | tf_op jit(solution)/shard_map/channel_sums/pallas_call | solution.py:192
  6.5 18.8 %all_to_all.20.rcv_ref = bf16[32,40,128]{2,1,0:T(8,128)(2,1)S(1)} all-to-all(bf16[32,40,128]{2,1,0:T(8,128)(2,1)S(1)} %get-tuple-element.12), channel_id=1, replica_groups=mesh['row'=2,'col'=4,'freq'=4] {'row','col','freq'}, dimensions={0} | all-to-all | bytes 655360 | tf_op jit(solution)/shard_map/all_to_all | solution.py:202
  25.3 0.0 copy-done
  25.4 0.0 copy-done.1
  25.4 5.0 %weighting.1 = (bf16[32,40,128]{2,1,0:T(8,128)(2,1)S(1)}, f32[32,1024]{1,0:T(8,128)S(1)}, f32[32,32]{1,0:T(8,128)S(1)}, f32[32,32]{1,0:T(8,128)S(1)}) custom-call(bf16[32,40,128]{2,1,0:T(8,128)(2,1)S(1)} %all_to_all.20.rcv_ref, s32[32]{0:T(128)S(1)} %copy-done.1, f32[32,1024]{1,0:T(8,128)S(1)} %get-tuple-element.13.taper_ref, bf16[512,1024]{1,0:T(8,128)(2,1)S(1)} %copy-done), custom_call_target="tpu_custom_call" | custom-call | tf_op jit(solution)/shard_map/weighting/pallas_call | solution.py:269
  30.4 14.0 %all_to_all.21.rcv_ref = bf16[32,40,128]{2,1,0:T(8,128)(2,1)S(1)} all-to-all(bf16[32,40,128]{2,1,0:T(8,128)(2,1)S(1)} %get-tuple-element.14), channel_id=1, replica_groups=mesh['row'=2,'col'=4,'freq'=4] {'row','col','freq'}, dimensions={0} | all-to-all | bytes 655360 | tf_op jit(solution)/shard_map/all_to_all | solution.py:283
  44.4 3.4 %contraction.1.p0 = bf16[32,512]{1,0:T(8,128)(2,1)S(1)} custom-call(bf16[512,16896]{1,0:T(8,128)(2,1)} %signal_ref.5, bf16[32,40,128]{2,1,0:T(8,128)(2,1)S(1)} %all_to_all.21.rcv_ref, f32[32,32]{1,0:T(8,128)S(1)} %get-tuple-element.15.inverse_ref), custom_call_target="tpu_custom_call" | custom-call | tf_op jit(solution)/shard_map/contraction/pallas_call | solution.py:296
  47.8 0.6 collective-permute-start.2
  48.4 1.1 %collective-permute-start.1 = (bf16[32,512]{1,0:T(8,128)(2,1)S(1)}, bf16[32,512]{1,0:T(8,128)(2,1)S(1)}, u32[]{:S(2)}, u32[]{:S(2)}) collective-permute-start(bf16[32,512]{1,0:T(8,128)(2,1)S(1)} %contraction.1.p0), channel_id=1, source_target_pairs={{0,2},{1,3},{2,0},{3,1},{4,6},{5,7},{6,4},{7,5},{8,10},{9,11},{10,... | collective-permute-start | bytes 98312 | tf_op jit(solution)/shard_map/ppermute | solution.py:306
  49.5 0.3 collective-permute-start
  49.7 1.7 %collective-permute-done.2.p3 = bf16[32,512]{1,0:T(8,128)(2,1)S(1)} collective-permute-done((bf16[32,512]{1,0:T(8,128)(2,1)S(1)}, bf16[32,512]{1,0:T(8,128)(2,1)S(1)}, u32[]{:S(2)}, u32[]{:S(2)}) %collective-permute-start.2) | collective-permute-done | bytes 32800 | tf_op jit(solution)/shard_map/ppermute | solution.py:306
  51.4 1.1 %collective-permute-done.1.p2 = bf16[32,512]{1,0:T(8,128)(2,1)S(1)} collective-permute-done((bf16[32,512]{1,0:T(8,128)(2,1)S(1)}, bf16[32,512]{1,0:T(8,128)(2,1)S(1)}, u32[]{:S(2)}, u32[]{:S(2)}) %collective-permute-start.1) | collective-permute-done | bytes 32800 | tf_op jit(solution)/shard_map/ppermute | solution.py:306
  52.5 0.0 collective-permute-done.p1
  52.5 2.9 %image_sums.1 = (f32[512,32]{1,0:T(8,128)S(1)}, bf16[32,40,128]{2,1,0:T(8,128)(2,1)S(1)}) custom-call(bf16[512,16896]{1,0:T(8,128)(2,1)} %signal_ref.5, bf16[32,512]{1,0:T(8,128)(2,1)S(1)} %contraction.1.p0, bf16[32,512]{1,0:T(8,128)(2,1)S(1)} %collective-permute-done.p1, bf16[32,512]{1,0:T(8,128)(2,1)S(1)} %collective-permute-done.1.p2, ...), custom_call_target="tpu_custom_call" | custom-call | tf_op jit(solution)/shard_map/image_sums/pallas_call | solution.py:322
  55.5 13.7 %all_to_all.22.rcv_ref = bf16[32,40,128]{2,1,0:T(8,128)(2,1)S(1)} all-to-all(bf16[32,40,128]{2,1,0:T(8,128)(2,1)S(1)} %get-tuple-element.17), channel_id=1, replica_groups=mesh['row'=2,'col'=4,'freq'=4] {'row','col','freq'}, dimensions={0} | all-to-all | bytes 655360 | tf_op jit(solution)/shard_map/all_to_all | solution.py:332
  69.1 5.2 %frequency_terms.1 = (f32[32,1,128]{2,1,0:T(1,128)}, f32[32,32]{1,0:T(8,128)S(1)}) custom-call(bf16[32,40,128]{2,1,0:T(8,128)(2,1)S(1)} %all_to_all.22.rcv_ref, s32[32]{0:T(128)S(1)} %copy-done.1, f32[32,1024]{1,0:T(8,128)S(1)} %get-tuple-element.13.taper_ref, bf16[512,1024]{1,0:T(8,128)(2,1)S(1)} %copy-done, f32[32,1024]{1,0:T(8,128)S(1)} %get-tuple-element.18.summed_ref, ...), custom_call_target="tpu_custom_call" | custom-call | tf_op jit(solution)/shard_map/frequency_terms/pallas_call | solution.py:347
  74.3 2.5 %all-to-all-start.3 = ((f32[32,1,128]{2,1,0:T(1,128)}), f32[32,1,128]{2,1,0:T(1,128)S(1)}, u32[]{:S(2)}, u32[]{:S(2)}) async-start(f32[32,1,128]{2,1,0:T(1,128)} %get-tuple-element.20), calls=%async_computation.3 | async-start | bytes 32768 | tf_op jit(solution)/shard_map/all_to_all | solution.py:360
  76.9 0.7 copy.10
  77.6 6.3 %all-to-all-done.3.terms_ref = f32[32,1,128]{2,1,0:T(1,128)S(1)} async-done(((f32[32,1,128]{2,1,0:T(1,128)}), f32[32,1,128]{2,1,0:T(1,128)S(1)}, u32[]{:S(2)}, u32[]{:S(2)}) %all-to-all-start.3) | async-done | bytes 16416 | tf_op jit(solution)/shard_map/all_to_all | solution.py:360
  83.9 0.3 frequency_solve.1
  84.2 0.7 copy.11
Async XLA Ops:
  0.6 24.7 %copy-start = (bf16[512,1024]{1,0:T(8,128)(2,1)S(1)}, bf16[512,1024]{1,0:T(8,128)(2,1)}, u32[]{:S(2)}) copy-start(bf16[512,1024]{1,0:T(8,128)(2,1)} %constant.3.table_ref) | copy-start | bytes 3145732
  0.6 24.7 %copy-start.1 = (s32[32]{0:T(128)S(1)}, s32[32]{0:T(128)}, u32[]{:S(2)}) copy-start(s32[32]{0:T(128)} %starts_ref.3) | copy-start | bytes 388
  2.4 0.7 copy-start.2
  47.8 3.6 %collective-permute-start.2 = (bf16[32,512]{1,0:T(8,128)(2,1)S(1)}, bf16[32,512]{1,0:T(8,128)(2,1)S(1)}, u32[]{:S(2)}, u32[]{:S(2)}) collective-permute-start(bf16[32,512]{1,0:T(8,128)(2,1)S(1)} %contraction.1.p0), channel_id=1, source_target_pairs={{0,3},{1,2},{2,1},{3,0},{4,7},{5,6},{6,5},{7,4},{8,11},{9,10},{10,... | collective-permute-start | bytes 98312 | tf_op jit(solution)/shard_map/ppermute | solution.py:306
  48.4 4.1 %collective-permute-start.1 = (bf16[32,512]{1,0:T(8,128)(2,1)S(1)}, bf16[32,512]{1,0:T(8,128)(2,1)S(1)}, u32[]{:S(2)}, u32[]{:S(2)}) collective-permute-start(bf16[32,512]{1,0:T(8,128)(2,1)S(1)} %contraction.1.p0), channel_id=1, source_target_pairs={{0,2},{1,3},{2,0},{3,1},{4,6},{5,7},{6,4},{7,5},{8,10},{9,11},{10,... | collective-permute-start | bytes 98312 | tf_op jit(solution)/shard_map/ppermute | solution.py:306
  49.5 3.1 %collective-permute-start = (bf16[32,512]{1,0:T(8,128)(2,1)S(1)}, bf16[32,512]{1,0:T(8,128)(2,1)S(1)}, u32[]{:S(2)}, u32[]{:S(2)}) collective-permute-start(bf16[32,512]{1,0:T(8,128)(2,1)S(1)} %contraction.1.p0), channel_id=1, source_target_pairs={{0,1},{1,0},{2,3},{3,2},{4,5},{5,4},{6,7},{7,6},{8,9},{9,8},{10,11... | collective-permute-start | bytes 98312 | tf_op jit(solution)/shard_map/ppermute | solution.py:306
  74.3 9.6 %all-to-all-start.3 = ((f32[32,1,128]{2,1,0:T(1,128)}), f32[32,1,128]{2,1,0:T(1,128)S(1)}, u32[]{:S(2)}, u32[]{:S(2)}) async-start(f32[32,1,128]{2,1,0:T(1,128)} %get-tuple-element.20), calls=%async_computation.3 | async-start | bytes 32768 | tf_op jit(solution)/shard_map/all_to_all | solution.py:360

commit v2 on v1

--- a/solution.py
+++ b/solution.py
@@ -14,7 +14,7 @@
 F32 = jnp.float32
 BF16 = jnp.bfloat16
 HIGHEST = lax.Precision.HIGHEST
-VMEM_BYTES = 48 << 20
+VMEM_BYTES = 16 << 20
 
 
 def half_table():
@@ -130,75 +130,112 @@
     total_rows = rows * nq
     freq_row, b_row, w_row = rows, rows + 1, rows + 5
     msg_rows = rows + 7
-    chunks = 3
-    chunk = span // chunks
+    third = rows // 3
+    held_spans = [(0, third), (third, third), (2 * third, rows - 2 * third)]
+    first_spans = [(i, min(8, rows - i)) for i in range(0, rows, 8)]
     assert rank == 32 and nq == 4 and bins == LANES and ndev >= rank and nc % 8 == 0
-    assert span % (chunks * LANES) == 0 and msg_rows % 8 == 0
+    assert span % LANES == 0 and msg_rows % 8 == 0
 
     vmem = pl.BlockSpec(memory_space=pltpu.VMEM)
     smem = pl.BlockSpec(memory_space=pltpu.SMEM)
-    hbm = pl.BlockSpec(memory_space=pl.ANY)
+    hbm = pl.BlockSpec(memory_space=pltpu.HBM)
     params = pltpu.CompilerParams(vmem_limit_bytes=VMEM_BYTES)
     table = half_table()
+    pinned = [
+        pltpu.with_memory_space_constraint(x, pltpu.HBM)
+        for x in (signal, chan_factor.T, freq_factor.T, win_len)
+    ]
     msg = jax.ShapeDtypeStruct((ndev, msg_rows, LANES), BF16)
 
-    def fetch(signal_ref, buf, sem):
+    def fetch(signal_ref, spans, bufs, sem):
         base = lax.axis_index("freq") * span
         copies = []
-        for i in range(chunks):
-            where = pl.multiple_of(base + i * chunk, LANES)
-            copies.append(
-                pltpu.make_async_copy(
-                    signal_ref.at[:, pl.ds(where, chunk)], buf.at[i], sem.at[i]
-                )
-            )
+        for i, ((first, count), buf) in enumerate(zip(spans, bufs)):
+            where = pl.multiple_of(base + first * LANES, LANES)
+            source = signal_ref.at[:, pl.ds(where, count * LANES)]
+            copies.append(pltpu.make_async_copy(source, buf, sem.at[i]))
         for copy in copies:
             copy.start()
         return copies
 
-    signal_scratch = [
-        pltpu.VMEM((chunks, chans, chunk), BF16),
-        pltpu.SemaphoreType.DMA((chunks,)),
-    ]
-
-    def channel_sums(lhs, copies, buf, out_ref):
-        if ndev > rank:
-            out_ref[...] = jnp.zeros_like(out_ref)
-        for i in range(chunks):
-            copies[i].wait()
-            part = dot(lhs, buf[i])
-            for j in range(chunk // LANES):
-                out_ref[:rank, i * (chunk // LANES) + j, :] = part[:, j * LANES : (j + 1) * LANES]
-
-    def sums_kernel(signal_ref, win_ref, chan_ref, freq_ref, msg_ref, taper_ref, buf, sem, out, gs):
-        copies = fetch(signal_ref, buf, sem)
+    def channel_sums(lhs, spans, bufs, copies, out_ref):
+        for i, (first, count) in enumerate(spans):
+            if copies is not None:
+                copies[i].wait()
+            part = dot(lhs, bufs[i][...])
+            for j in range(count):
+                out_ref[:rank, first + j, :] = part[:, j * LANES : (j + 1) * LANES]
+
+    def sums_kernel(
+        signal_ref, chan_hbm, freq_hbm, win_hbm, msg_ref, taper_ref,
+        buf, sem, chan_ref, freq_ref, win_ref, small, out, gs,
+    ):
+        small_copies = [
+            pltpu.make_async_copy(chan_hbm, chan_ref, small.at[0]),
+            pltpu.make_async_copy(freq_hbm, freq_ref, small.at[1]),
+            pltpu.make_async_copy(win_hbm, win_ref, small.at[2]),
+        ]
+        for copy in small_copies:
+            copy.start()
+        bufs = [buf.at[:, a * LANES : (a + n) * LANES] for a, n in first_spans]
+        copies = fetch(signal_ref, first_spans, bufs, sem)
         q = lax.axis_index("freq")
         c = lax.axis_index("row") * mesh_size["col"] + lax.axis_index("col")
-        taper_ref[...] = taper_of(win_ref)
-        chan = chan_ref[...].astype(F32).T
-        chan_low = chan.astype(BF16)
-        weights = freq_ref[...].astype(F32).T
-        channel_sums(chan_low, copies, buf, out)
-        out[:rank, freq_row, :] = weights
+        if ndev > rank:
+            out[...] = jnp.zeros_like(out)
+        for copy in small_copies:
+            copy.wait()
+        chan_low = chan_ref[...]
+        weights_low = freq_ref[...]
+        out[:rank, freq_row, :] = weights_low.astype(F32)
         gs[...] = split_rows(dot(chan_low, chan_low, ((1,), (1,))), rank)
         side = packed_side(gs, q * 8, 4)
         out[:, b_row : b_row + 4, :] = jnp.broadcast_to(side[None], (ndev, 4, LANES))
-        weights_low = weights.astype(BF16)
         gs[...] = split_rows(dot(weights_low, weights_low, ((1,), (1,))), rank)
         side = packed_side(gs, (c % 8) * 4, 2)
         out[:, w_row : w_row + 2, :] = jnp.broadcast_to(side[None], (ndev, 2, LANES))
+        taper_ref[...] = taper_of(win_ref)
+        channel_sums(chan_low, first_spans, bufs, copies, out)
         msg_ref[...] = out[...].astype(BF16)
 
     message, taper = pl.pallas_call(
         sums_kernel,
         out_shape=(msg, jax.ShapeDtypeStruct((SEGS, NW), F32)),
-        in_specs=[hbm, smem, vmem, vmem],
+        in_specs=[hbm] * 4,
         out_specs=(vmem, vmem),
-        scratch_shapes=signal_scratch
-        + [pltpu.VMEM((ndev, msg_rows, LANES), F32), pltpu.VMEM((rank, LANES), F32)],
+        scratch_shapes=[
+            pltpu.VMEM((chans, span), BF16),
+            pltpu.SemaphoreType.DMA((len(first_spans),)),
+            pltpu.VMEM((rank, chans), BF16),
+            pltpu.VMEM((rank, bins), BF16),
+            pltpu.SMEM((SEGS,), jnp.int32),
+            pltpu.SemaphoreType.DMA((3,)),
+            pltpu.VMEM((ndev, msg_rows, LANES), F32),
+            pltpu.VMEM((rank, LANES), F32),
+        ],
         compiler_params=params,
         name="channel_sums",
-    )(signal, win_len, chan_factor, freq_factor)
+    )(*pinned)
+
+    def hold_kernel(signal_ref, gram_ref, buf0, buf1, inverse_ref, sem):
+        copies = fetch(signal_ref, held_spans[:2], (buf0, buf1), sem)
+        inverse_ref[...] = spd_inverse(gram_ref[...])
+        for copy in copies:
+            copy.wait()
+
+    def inverse_kernel(gram_ref, inverse_ref):
+        inverse_ref[...] = spd_inverse(gram_ref[...])
+
+    def inverse_of(gram):
+        return pl.pallas_call(
+            inverse_kernel,
+            out_shape=jax.ShapeDtypeStruct(gram.shape, F32),
+            in_specs=[vmem],
+            out_specs=vmem,
+            compiler_params=params,
+            name="inverse",
+        )(gram)
+
     received = lax.all_to_all(message, ALL, 0, 0, tiled=True)
 
     z_rows = (total_rows + 8 + 7) // 8 * 8
@@ -216,7 +253,7 @@
 
     def weight_kernel(
         rcv_ref, starts_ref, taper_ref, table_ref,
-        msg_ref, summed_ref, inverse_ref, gram_ref,
+        msg_ref, summed_ref, system_ref, gram_ref,
         z_ref, y_ref, gs, u_ref,
     ):
         gram_b = gather_rank(rcv_ref, z_ref, gs)
@@ -228,7 +265,7 @@
             gs[4 * c : 4 * c + 2, :] = side
             gs[4 * c + 2 : 4 * c + 4, :] = side
         gram_w = join_rows(gs, 4)
-        inverse_ref[...] = spd_inverse(gram_b * gram_w)
+        system_ref[...] = gram_b * gram_w
         taper = taper_ref[...]
         table = table_ref[...]
         summed = forward(windows(z_ref, y_ref, starts_ref) * taper, table)
@@ -266,7 +303,7 @@
                 msg_ref[c * nq + q] = piece
 
     square = jax.ShapeDtypeStruct((rank, rank), F32)
-    message, summed, inverse, gram_b = pl.pallas_call(
+    message, summed, system, gram_b = pl.pallas_call(
         weight_kernel,
         out_shape=(msg, jax.ShapeDtypeStruct((SEGS, NW), F32), square, square),
         in_specs=[vmem, smem, vmem, vmem],
@@ -281,38 +318,55 @@
         name="weighting",
     )(received, starts, taper, table)
     received = lax.all_to_all(message, ALL, 0, 0, tiled=True)
-
-    def contract_kernel(signal_ref, rcv_ref, inverse_ref, part_ref, buf, sem, out):
-        copies = fetch(signal_ref, buf, sem)
+    pieces = [jax.ShapeDtypeStruct((chans, n * LANES), BF16) for _, n in held_spans]
+    *held, inverse = pl.pallas_call(
+        hold_kernel,
+        out_shape=(pieces[0], pieces[1], square),
+        in_specs=[hbm, vmem],
+        out_specs=(vmem,) * 3,
+        scratch_shapes=[pltpu.SemaphoreType.DMA((2,))],
+        compiler_params=params,
+        name="hold_signal",
+    )(pinned[0], system)
+
+    def contract_kernel(
+        signal_ref, buf0, buf1, rcv_ref, inverse_ref, part_ref, buf2, sem, out
+    ):
+        copies = fetch(signal_ref, held_spans[2:], (buf2,), sem)
         out[...] = rcv_ref[:rank].astype(F32)
         total = jnp.zeros((rank, chans), F32)
-        for i in range(chunks):
-            pieces = [out[:, i * (chunk // LANES) + j, :] for j in range(chunk // LANES)]
-            operand = jnp.concatenate(pieces, axis=1).astype(BF16)
-            copies[i].wait()
-            total = total + dot(operand, buf[i], ((1,), (1,)))
+        for (first, count), buf in zip(held_spans, (buf0, buf1, buf2)):
+            columns = [out[:, first + j, :] for j in range(count)]
+            operand = jnp.concatenate(columns, axis=1).astype(BF16)
+            if buf is buf2:
+                copies[0].wait()
+            total = total + dot(operand, buf[...], ((1,), (1,)))
         part_ref[...] = dot(inverse_ref[...], total, precision=HIGHEST).astype(BF16)
 
-    part = pl.pallas_call(
+    part, last = pl.pallas_call(
         contract_kernel,
-        out_shape=jax.ShapeDtypeStruct((rank, chans), BF16),
-        in_specs=[hbm, vmem, vmem],
-        out_specs=vmem,
-        scratch_shapes=signal_scratch + [pltpu.VMEM((rank, msg_rows, LANES), F32)],
+        out_shape=(jax.ShapeDtypeStruct((rank, chans), BF16), pieces[2]),
+        in_specs=[hbm] + [vmem] * 4,
+        out_specs=(vmem, vmem),
+        scratch_shapes=[
+            pltpu.SemaphoreType.DMA((1,)),
+            pltpu.VMEM((rank, msg_rows, LANES), F32),
+        ],
         compiler_params=params,
         name="contraction",
-    )(signal, received, inverse)
+    )(pinned[0], *held, received, inverse)
     parts = [part] + [
         lax.ppermute(part, "freq", [(i, i ^ m) for i in range(nq)]) for m in range(1, nq)
     ]
 
-    def images_kernel(signal_ref, p0, p1, p2, p3, chan_ref, msg_ref, buf, sem, out, gs):
-        copies = fetch(signal_ref, buf, sem)
+    def images_kernel(buf0, buf1, buf2, p0, p1, p2, p3, chan_ref, msg_ref, out, gs):
         q = lax.axis_index("freq")
         pair = p0[...].astype(F32) + p1[...].astype(F32)
         new_chan = pair + (p2[...].astype(F32) + p3[...].astype(F32))
-        chan_ref[...] = new_chan.T
-        channel_sums(new_chan.astype(BF16), copies, buf, out)
+        chan_ref[...] = new_chan
+        if ndev > rank:
+            out[...] = jnp.zeros_like(out)
+        channel_sums(new_chan.astype(BF16), held_spans, (buf0, buf1, buf2), None, out)
         gs[...] = split_rows(dot(new_chan, new_chan, ((1,), (1,)), HIGHEST), rank)
         side = packed_side(gs, q * 8, 4)
         out[:, freq_row:, :] = jnp.zeros((ndev, msg_rows - rows, LANES), F32)
@@ -321,22 +375,21 @@
 
     new_chan, message = pl.pallas_call(
         images_kernel,
-        out_shape=(jax.ShapeDtypeStruct((chans, rank), F32), msg),
-        in_specs=[hbm] + [vmem] * 4,
+        out_shape=(jax.ShapeDtypeStruct((rank, chans), F32), msg),
+        in_specs=[vmem] * 7,
         out_specs=(vmem, vmem),
-        scratch_shapes=signal_scratch
-        + [pltpu.VMEM((ndev, msg_rows, LANES), F32), pltpu.VMEM((rank, LANES), F32)],
+        scratch_shapes=[pltpu.VMEM((ndev, msg_rows, LANES), F32), pltpu.VMEM((rank, LANES), F32)],
         compiler_params=params,
         name="image_sums",
-    )(signal, *parts)
+    )(*held, last, *parts)
     received = lax.all_to_all(message, ALL, 0, 0, tiled=True)
 
     def terms_kernel(
         rcv_ref, starts_ref, taper_ref, table_ref, summed_ref, gram_ref,
-        terms_ref, inverse_ref, z_ref, y_ref, gs,
+        terms_ref, system_ref, z_ref, y_ref, gs,
     ):
         gram_a = gather_rank(rcv_ref, z_ref, gs)
-        inverse_ref[...] = spd_inverse(gram_a * gram_ref[...])
+        system_ref[...] = gram_a * gram_ref[...]
         images = forward(windows(z_ref, y_ref, starts_ref) * taper_ref[...], table_ref[...])
         terms = jnp.sum(images * summed_ref[...], axis=0, keepdims=True) / SEGS
         terms = terms[:, :HALF] + terms[:, HALF:]
@@ -344,7 +397,7 @@
             q = d % nq
             terms_ref[d] = terms[:, q * bins : (q + 1) * bins]
 
-    terms, inverse = pl.pallas_call(
+    terms, system = pl.pallas_call(
         terms_kernel,
         out_shape=(jax.ShapeDtypeStruct((ndev, 1, bins), F32), square),
         in_specs=[vmem, smem, vmem, vmem, vmem, vmem],
@@ -358,20 +411,21 @@
         name="frequency_terms",
     )(received, starts, taper, table, summed, gram_b)
     terms = lax.all_to_all(terms, ALL, 0, 0, tiled=True)
+    inverse = inverse_of(system)
 
     def finish_kernel(terms_ref, inverse_ref, out_ref):
         gathered = terms_ref[:rank, 0, :]
-        out_ref[...] = dot(gathered, inverse_ref[...], ((0,), (0,)), HIGHEST)
+        out_ref[...] = dot(inverse_ref[...], gathered, precision=HIGHEST)
 
     new_freq = pl.pallas_call(
         finish_kernel,
-        out_shape=jax.ShapeDtypeStruct((bins, rank), F32),
+        out_shape=jax.ShapeDtypeStruct((rank, bins), F32),
         in_specs=[vmem, vmem],
         out_specs=vmem,
         compiler_params=params,
         name="frequency_solve",
     )(terms, inverse)
-    return (new_chan, new_freq)
+    return (new_chan.T, new_freq.T)
 
 
 def solution(mesh):

time: 85.2 us -> 74.6 us (0.88)
  blocking collectives: 46.5 us -> 32.4 us
  local copies, waits for them, and re-layouts: 3.86 us -> 0.01 us
  waiting for transfers between devices: 9.12 us -> 12.2 us
  starting transfers between devices: 4.47 us -> 7.06 us
  Pallas kernels: 20.3 us -> 22 us
    all_to_all x3 -> x2, blocking collectives: 46.5 us -> 32.4 us  [body(): received = lax.all_to_all(message, ALL, 0, 0, tiled=True)]
    pallas_call x3 -> x5, Pallas kernels: 6.62 us -> 13.9 us  [the longest x1 5.4 us: body(): pl.pallas_call(hold_kernel, out_shape=(pieces[0], pieces[1], square), in_...]
    all_to_all x0 -> x1, waiting for transfers between devices: none -> 6.29 us  [body(): received = lax.all_to_all(message, ALL, 0, 0, tiled=True)]
    unnamed x10 -> x6, local copies, waits for them, and re-layouts: 3.86 us -> 0.01 us
    pallas_call x1, Pallas kernels: 5.19 us -> 1.79 us  [body(): pl.pallas_call(terms_kernel, out_shape=(jax.ShapeDtypeStruct((ndev, 1, bi...]
    all_to_all x1, waiting for transfers between devices: 6.33 us -> 3.09 us  [body(): terms = lax.all_to_all(terms, ALL, 0, 0, tiled=True)]
    all_to_all x0 -> x1, starting transfers between devices: none -> 2.59 us  [body(): received = lax.all_to_all(message, ALL, 0, 0, tiled=True)]
    pallas_call x1, Pallas kernels: 5.02 us -> 2.65 us  [body(): pl.pallas_call(weight_kernel, out_shape=(msg, jax.ShapeDtypeStruct((SEGS,...]
  transfers between devices with their start and end apart: 4 -> 5, of which waited for: 3 -> 4; matrix products, arithmetic and copies ran while one was open for 1% -> 0% of each run, Pallas kernels for 0% -> 13%
where the time goes in v2:
time: 74.6 us; the launch traced here: 74.3 us
  blocking collectives  32.4 us (43%)
  Pallas kernels  22 us (29%)
  waiting for transfers between devices  12.2 us (16%)
  starting transfers between devices  7.06 us (9%)
    all_to_all x2, blocking collectives, body(): received = lax.all_to_all(message, ALL, 0, 0, tiled=True)  32.4 us
    all_to_all x1, waiting for transfers between devices, body(): received = lax.all_to_all(message, ALL, 0, 0, tiled=True)  6.29 us
    pallas_call x1, Pallas kernels, body(): pl.pallas_call(hold_kernel, out_shape=(pieces[0], pieces[1], square), in_...  5.4 us
    pallas_call x1, Pallas kernels, inverse_of(): pl.pallas_call(inverse_kernel, out_shape=jax.ShapeDtypeStruct(gram.shape,...  3.98 us
    pallas_call x1, Pallas kernels, body(): pl.pallas_call(sums_kernel, out_shape=(msg, jax.ShapeDtypeStruct((SEGS, N...  3.68 us
    all_to_all x1, waiting for transfers between devices, body(): terms = lax.all_to_all(terms, ALL, 0, 0, tiled=True)  3.09 us
    ppermute x3, waiting for transfers between devices, body(): lax.ppermute(part, 'freq', [(i, i ^ m) for i in range(nq)])  2.78 us
    pallas_call x1, Pallas kernels, body(): pl.pallas_call(weight_kernel, out_shape=(msg, jax.ShapeDtypeStruct((SEGS,...  2.65 us
  transfers between devices with their start and end apart: 5, of which 4 were waited for; matrix products, arithmetic and copies ran while one was open for 0% of the time, Pallas kernels for 13%

profile of v2, /device:TPU:0, one launch (start us, length us, event | category | flops | bytes accessed | tf_op | source)
XLA Modules:
  0.0 74.3 jit_solution(16899733805376343017)
XLA Ops:
  0.6 0.0 copy-start
  0.6 0.0 copy-start.2
  0.7 3.7 %channel_sums.1 = (bf16[32,40,128]{2,1,0:T(8,128)(2,1)S(1)}, f32[32,1024]{1,0:T(8,128)S(1)}) custom-call(bf16[512,16896]{1,0:T(8,128)(2,1)} %signal_ref.5, bf16[32,512]{1,0:T(8,128)(2,1)} %bitcast.4, bf16[32,128]{1,0:T(8,128)(2,1)} %bitcast.6, s32[32]{0:T(128)} %win_hbm.1), custom_call_target="tpu_custom_call" | custom-call | tf_op jit(solution)/shard_map/channel_sums/pallas_call | solution.py:201
  4.3 18.8 %all_to_all.20.rcv_ref = bf16[32,40,128]{2,1,0:T(8,128)(2,1)S(1)} all-to-all(bf16[32,40,128]{2,1,0:T(8,128)(2,1)S(1)} %get-tuple-element.17), channel_id=1, replica_groups=mesh['row'=2,'col'=4,'freq'=4] {'row','col','freq'}, dimensions={0} | all-to-all | bytes 655360 | tf_op jit(solution)/shard_map/all_to_all | solution.py:239
  23.1 0.0 copy-done
  23.2 0.0 copy-done.2
  23.2 2.7 %weighting.1 = (bf16[32,40,128]{2,1,0:T(8,128)(2,1)}, f32[32,1024]{1,0:T(8,128)S(1)}, f32[32,32]{1,0:T(8,128)S(1)}, f32[32,32]{1,0:T(8,128)S(1)}) custom-call(bf16[32,40,128]{2,1,0:T(8,128)(2,1)S(1)} %all_to_all.20.rcv_ref, s32[32]{0:T(128)S(1)} %copy-done.2, f32[32,1024]{1,0:T(8,128)S(1)} %get-tuple-element.18.taper_ref, bf16[512,1024]{1,0:T(8,128)(2,1)S(1)} %copy-done), custom_call_target="tpu_custom_call" | custom-call | tf_op jit(solution)/shard_map/weighting/pallas_call | solution.py:306
  25.8 2.6 %all-to-all-start.1 = ((bf16[32,40,128]{2,1,0:T(8,128)(2,1)}), bf16[32,40,128]{2,1,0:T(8,128)(2,1)S(1)}, u32[]{:S(2)}, u32[]{:S(2)}) async-start(bf16[32,40,128]{2,1,0:T(8,128)(2,1)} %get-tuple-element.22), calls=%async_computation.1 | async-start | bytes 655360 | tf_op jit(solution)/shard_map/all_to_all | solution.py:320
  28.4 5.4 %hold_signal.1 = (bf16[512,1408]{1,0:T(8,128)(2,1)S(1)}, bf16[512,1408]{1,0:T(8,128)(2,1)S(1)}, f32[32,32]{1,0:T(8,128)S(1)}) custom-call(bf16[512,16896]{1,0:T(8,128)(2,1)} %signal_ref.5, f32[32,32]{1,0:T(8,128)S(1)} %get-tuple-element.19.gram_ref), custom_call_target="tpu_custom_call" | custom-call | tf_op jit(solution)/shard_map/hold_signal/pallas_call | solution.py:322
  33.8 6.3 %all-to-all-done.1.rcv_ref = bf16[32,40,128]{2,1,0:T(8,128)(2,1)S(1)} async-done(((bf16[32,40,128]{2,1,0:T(8,128)(2,1)}), bf16[32,40,128]{2,1,0:T(8,128)(2,1)S(1)}, u32[]{:S(2)}, u32[]{:S(2)}) %all-to-all-start.1) | async-done | bytes 327712 | tf_op jit(solution)/shard_map/all_to_all | solution.py:320
  40.1 2.6 %contraction.1 = (bf16[32,512]{1,0:T(8,128)(2,1)S(1)}, bf16[512,1408]{1,0:T(8,128)(2,1)S(1)}) custom-call(bf16[512,16896]{1,0:T(8,128)(2,1)} %signal_ref.5, bf16[512,1408]{1,0:T(8,128)(2,1)S(1)} %get-tuple-element.20.buf0, bf16[512,1408]{1,0:T(8,128)(2,1)S(1)} %get-tuple-element.21.buf1, bf16[32,40,128]{2,1,0:T(8,128)(2,1)S(1)} %all-to-all-done.1.rcv_ref, ...), custom_call_target="tpu_custom_call" | custom-call | tf_op jit(solution)/shard_map/contraction/pallas_call | solution.py:346
  42.7 0.6 collective-permute-start.2
  43.3 1.1 %collective-permute-start.1 = (bf16[32,512]{1,0:T(8,128)(2,1)S(1)}, bf16[32,512]{1,0:T(8,128)(2,1)S(1)}, u32[]{:S(2)}, u32[]{:S(2)}) collective-permute-start(bf16[32,512]{1,0:T(8,128)(2,1)S(1)} %get-tuple-element.25.p0), channel_id=1, source_target_pairs={{0,2},{1,3},{2,0},{3,1},{4,6},{5,7},{6,4},{7,5},{8,10},{9,11},{10,... | collective-permute-start | bytes 98312 | tf_op jit(solution)/shard_map/ppermute | solution.py:359
  44.4 0.3 collective-permute-start
  44.7 1.7 %collective-permute-done.2.p3 = bf16[32,512]{1,0:T(8,128)(2,1)S(1)} collective-permute-done((bf16[32,512]{1,0:T(8,128)(2,1)S(1)}, bf16[32,512]{1,0:T(8,128)(2,1)S(1)}, u32[]{:S(2)}, u32[]{:S(2)}) %collective-permute-start.2) | collective-permute-done | bytes 32800 | tf_op jit(solution)/shard_map/ppermute | solution.py:359
  46.4 1.1 %collective-permute-done.1.p2 = bf16[32,512]{1,0:T(8,128)(2,1)S(1)} collective-permute-done((bf16[32,512]{1,0:T(8,128)(2,1)S(1)}, bf16[32,512]{1,0:T(8,128)(2,1)S(1)}, u32[]{:S(2)}, u32[]{:S(2)}) %collective-permute-start.1) | collective-permute-done | bytes 32800 | tf_op jit(solution)/shard_map/ppermute | solution.py:359
  47.4 0.0 collective-permute-done.p1
  47.4 0.0 copy-start.1
  47.4 1.1 %image_sums.1 = (f32[32,512]{1,0:T(8,128)}, bf16[32,40,128]{2,1,0:T(8,128)(2,1)S(1)}) custom-call(bf16[512,1408]{1,0:T(8,128)(2,1)S(1)} %get-tuple-element.20.buf0, bf16[512,1408]{1,0:T(8,128)(2,1)S(1)} %get-tuple-element.21.buf1, bf16[512,1408]{1,0:T(8,128)(2,1)S(1)} %get-tuple-element.24.buf2, bf16[32,512]{1,0:T(8,128)(2,1)S(1)} %get-tuple-element.25.p0, ...), custom_call_target="tpu_custom_call" | custom-call | tf_op jit(solution)/shard_map/image_sums/pallas_call | solution.py:376
  48.6 13.6 %all_to_all.21.rcv_ref = bf16[32,40,128]{2,1,0:T(8,128)(2,1)S(1)} all-to-all(bf16[32,40,128]{2,1,0:T(8,128)(2,1)S(1)} %get-tuple-element.27), channel_id=1, replica_groups=mesh['row'=2,'col'=4,'freq'=4] {'row','col','freq'}, dimensions={0} | all-to-all | bytes 655360 | tf_op jit(solution)/shard_map/all_to_all | solution.py:385
  62.1 0.0 copy-done.1
  62.1 1.8 %frequency_terms.1 = (f32[32,1,128]{2,1,0:T(1,128)}, f32[32,32]{1,0:T(8,128)S(1)}) custom-call(bf16[32,40,128]{2,1,0:T(8,128)(2,1)S(1)} %all_to_all.21.rcv_ref, s32[32]{0:T(128)S(1)} %copy-done.2, f32[32,1024]{1,0:T(8,128)S(1)} %get-tuple-element.18.taper_ref, bf16[512,1024]{1,0:T(8,128)(2,1)S(1)} %copy-done.1, f32[32,1024]{1,0:T(8,128)S(1)} %get-tuple-element.28.summed_ref, ...), custom_call_target="tpu_custom_call" | custom-call | tf_op jit(solution)/shard_map/frequency_terms/pallas_call | solution.py:400
  63.9 2.5 %all-to-all-start.3 = ((f32[32,1,128]{2,1,0:T(1,128)}), f32[32,1,128]{2,1,0:T(1,128)S(1)}, u32[]{:S(2)}, u32[]{:S(2)}) async-start(f32[32,1,128]{2,1,0:T(1,128)} %get-tuple-element.30), calls=%async_computation.3 | async-start | bytes 32768 | tf_op jit(solution)/shard_map/all_to_all | solution.py:413
  66.5 4.0 %inverse.1.inverse_ref = f32[32,32]{1,0:T(8,128)S(1)} custom-call(f32[32,32]{1,0:T(8,128)S(1)} %get-tuple-element.31.gram_ref), custom_call_target="tpu_custom_call" | custom-call | tf_op jit(solution)/shard_map/inverse/pallas_call | solution.py:230
  70.4 3.1 %all-to-all-done.3.terms_ref = f32[32,1,128]{2,1,0:T(1,128)S(1)} async-done(((f32[32,1,128]{2,1,0:T(1,128)}), f32[32,1,128]{2,1,0:T(1,128)S(1)}, u32[]{:S(2)}, u32[]{:S(2)}) %all-to-all-start.3) | async-done | bytes 16416 | tf_op jit(solution)/shard_map/all_to_all | solution.py:413
  73.5 0.8 %frequency_solve.1 = f32[32,128]{1,0:T(8,128)} custom-call(f32[32,1,128]{2,1,0:T(1,128)S(1)} %all-to-all-done.3.terms_ref, f32[32,32]{1,0:T(8,128)S(1)} %inverse.1.inverse_ref), custom_call_target="tpu_custom_call" | custom-call | tf_op jit(solution)/shard_map/frequency_solve/pallas_call | solution.py:420
Async XLA Ops:
  0.6 22.5 %copy-start = (bf16[512,1024]{1,0:T(8,128)(2,1)S(1)}, bf16[512,1024]{1,0:T(8,128)(2,1)}, u32[]{:S(2)}) copy-start(bf16[512,1024]{1,0:T(8,128)(2,1)} %constant.3.table_ref) | copy-start | bytes 3145732
  0.6 22.5 %copy-start.2 = (s32[32]{0:T(128)S(1)}, s32[32]{0:T(128)}, u32[]{:S(2)}) copy-start(s32[32]{0:T(128)} %starts_ref.3) | copy-start | bytes 388
  25.8 14.3 %all-to-all-start.1 = ((bf16[32,40,128]{2,1,0:T(8,128)(2,1)}), bf16[32,40,128]{2,1,0:T(8,128)(2,1)S(1)}, u32[]{:S(2)}, u32[]{:S(2)}) async-start(bf16[32,40,128]{2,1,0:T(8,128)(2,1)} %get-tuple-element.22), calls=%async_computation.1 | async-start | bytes 655360 | tf_op jit(solution)/shard_map/all_to_all | solution.py:320
  42.7 3.6 %collective-permute-start.2 = (bf16[32,512]{1,0:T(8,128)(2,1)S(1)}, bf16[32,512]{1,0:T(8,128)(2,1)S(1)}, u32[]{:S(2)}, u32[]{:S(2)}) collective-permute-start(bf16[32,512]{1,0:T(8,128)(2,1)S(1)} %get-tuple-element.25.p0), channel_id=1, source_target_pairs={{0,3},{1,2},{2,1},{3,0},{4,7},{5,6},{6,5},{7,4},{8,11},{9,10},{10,... | collective-permute-start | bytes 98312 | tf_op jit(solution)/shard_map/ppermute | solution.py:359
  43.3 4.1 %collective-permute-start.1 = (bf16[32,512]{1,0:T(8,128)(2,1)S(1)}, bf16[32,512]{1,0:T(8,128)(2,1)S(1)}, u32[]{:S(2)}, u32[]{:S(2)}) collective-permute-start(bf16[32,512]{1,0:T(8,128)(2,1)S(1)} %get-tuple-element.25.p0), channel_id=1, source_target_pairs={{0,2},{1,3},{2,0},{3,1},{4,6},{5,7},{6,4},{7,5},{8,10},{9,11},{10,... | collective-permute-start | bytes 98312 | tf_op jit(solution)/shard_map/ppermute | solution.py:359
  44.4 3.1 %collective-permute-start = (bf16[32,512]{1,0:T(8,128)(2,1)S(1)}, bf16[32,512]{1,0:T(8,128)(2,1)S(1)}, u32[]{:S(2)}, u32[]{:S(2)}) collective-permute-start(bf16[32,512]{1,0:T(8,128)(2,1)S(1)} %get-tuple-element.25.p0), channel_id=1, source_target_pairs={{0,1},{1,0},{2,3},{3,2},{4,5},{5,4},{6,7},{7,6},{8,9},{9,8},{10,11... | collective-permute-start | bytes 98312 | tf_op jit(solution)/shard_map/ppermute | solution.py:359
  47.4 14.7 %copy-start.1 = (bf16[512,1024]{1,0:T(8,128)(2,1)S(1)}, bf16[512,1024]{1,0:T(8,128)(2,1)}, u32[]{:S(2)}) copy-start(bf16[512,1024]{1,0:T(8,128)(2,1)} %constant.3.table_ref) | copy-start | bytes 3145732
  63.9 9.6 %all-to-all-start.3 = ((f32[32,1,128]{2,1,0:T(1,128)}), f32[32,1,128]{2,1,0:T(1,128)S(1)}, u32[]{:S(2)}, u32[]{:S(2)}) async-start(f32[32,1,128]{2,1,0:T(1,128)} %get-tuple-element.30), calls=%async_computation.3 | async-start | bytes 32768 | tf_op jit(solution)/shard_map/all_to_all | solution.py:413

commit v3 on v2

--- a/solution.py
+++ b/solution.py
@@ -15,6 +15,7 @@
 BF16 = jnp.bfloat16
 HIGHEST = lax.Precision.HIGHEST
 VMEM_BYTES = 16 << 20
+AHEAD = 8
 
 
 def half_table():
@@ -36,22 +37,20 @@
 
 def spd_inverse(system):
     size = system.shape[0]
-    rows, cols = iota((size, size), 0), iota((size, size), 1)
+    system = jnp.concatenate([system, jnp.zeros((size, LANES - size), F32)], axis=1)
+    rows, cols = iota((size, LANES), 0), iota((size, LANES), 1)
     for i in range(size):
-        row, col = system[i : i + 1, :], system[:, i : i + 1]
-        pivot = 1.0 / system[i : i + 1, i : i + 1]
-        scaled = row * pivot
-        here, there = rows == i, cols == i
-        updated = system - col * scaled
-        updated = jnp.where(there, col * pivot, updated)
-        updated = jnp.where(here, scaled, updated)
-        system = jnp.where(here & there, -pivot, updated)
-    return -system
-
-
-def split_rows(gram, size):
-    spread = (iota((size, LANES), 1) % size == iota((size, LANES), 0)).astype(F32)
-    tiled = dot(gram, spread, precision=HIGHEST)
+        col = jnp.broadcast_to(system[:, i : i + 1], (size, LANES))
+        pivot = 1.0 / col[i : i + 1]
+        scaled = jnp.where(cols[:1] == i, pivot, system[i : i + 1] * pivot)
+        cleared = jnp.where(cols == i, 0.0, system)
+        system = jnp.where(rows == i, scaled, cleared - col * scaled)
+    return system[:, :size]
+
+
+def split_gram(factor, precision=None):
+    size = factor.shape[0]
+    tiled = dot(factor, jnp.concatenate([factor] * 4, axis=0), ((1,), (1,)), precision)
     high = tiled.astype(BF16).astype(F32)
     return jnp.where(iota((size, LANES), 1) // size % 2 == 0, high, tiled - high)
 
@@ -132,7 +131,7 @@
     msg_rows = rows + 7
     third = rows // 3
     held_spans = [(0, third), (third, third), (2 * third, rows - 2 * third)]
-    first_spans = [(i, min(8, rows - i)) for i in range(0, rows, 8)]
+    first_spans = [(0, 12), (12, 12), (24, rows - 24)]
     assert rank == 32 and nq == 4 and bins == LANES and ndev >= rank and nc % 8 == 0
     assert span % LANES == 0 and msg_rows % 8 == 0
 
@@ -147,21 +146,23 @@
     ]
     msg = jax.ShapeDtypeStruct((ndev, msg_rows, LANES), BF16)
 
-    def fetch(signal_ref, spans, bufs, sem):
+    def fetch(signal_ref, spans, bufs, sem, ahead=8):
         base = lax.axis_index("freq") * span
         copies = []
         for i, ((first, count), buf) in enumerate(zip(spans, bufs)):
             where = pl.multiple_of(base + first * LANES, LANES)
             source = signal_ref.at[:, pl.ds(where, count * LANES)]
             copies.append(pltpu.make_async_copy(source, buf, sem.at[i]))
-        for copy in copies:
+        for copy in copies[:ahead]:
             copy.start()
         return copies
 
-    def channel_sums(lhs, spans, bufs, copies, out_ref):
+    def channel_sums(lhs, spans, bufs, copies, out_ref, ahead=8):
         for i, (first, count) in enumerate(spans):
-            if copies is not None:
+            if copies[i] is not None:
                 copies[i].wait()
+                if i + ahead < len(copies):
+                    copies[i + ahead].start()
             part = dot(lhs, bufs[i][...])
             for j in range(count):
                 out_ref[:rank, first + j, :] = part[:, j * LANES : (j + 1) * LANES]
@@ -178,24 +179,24 @@
         for copy in small_copies:
             copy.start()
         bufs = [buf.at[:, a * LANES : (a + n) * LANES] for a, n in first_spans]
-        copies = fetch(signal_ref, first_spans, bufs, sem)
+        copies = fetch(signal_ref, first_spans, bufs, sem, AHEAD)
         q = lax.axis_index("freq")
         c = lax.axis_index("row") * mesh_size["col"] + lax.axis_index("col")
         if ndev > rank:
             out[...] = jnp.zeros_like(out)
         for copy in small_copies:
             copy.wait()
+        taper_ref[...] = taper_of(win_ref)
         chan_low = chan_ref[...]
         weights_low = freq_ref[...]
         out[:rank, freq_row, :] = weights_low.astype(F32)
-        gs[...] = split_rows(dot(chan_low, chan_low, ((1,), (1,))), rank)
-        side = packed_side(gs, q * 8, 4)
+        gs[0] = split_gram(chan_low)
+        gs[1] = split_gram(weights_low)
+        channel_sums(chan_low, first_spans, bufs, copies, out, AHEAD)
+        side = packed_side(gs.at[0], q * 8, 4)
         out[:, b_row : b_row + 4, :] = jnp.broadcast_to(side[None], (ndev, 4, LANES))
-        gs[...] = split_rows(dot(weights_low, weights_low, ((1,), (1,))), rank)
-        side = packed_side(gs, (c % 8) * 4, 2)
+        side = packed_side(gs.at[1], (c % 8) * 4, 2)
         out[:, w_row : w_row + 2, :] = jnp.broadcast_to(side[None], (ndev, 2, LANES))
-        taper_ref[...] = taper_of(win_ref)
-        channel_sums(chan_low, first_spans, bufs, copies, out)
         msg_ref[...] = out[...].astype(BF16)
 
     message, taper = pl.pallas_call(
@@ -211,7 +212,7 @@
             pltpu.SMEM((SEGS,), jnp.int32),
             pltpu.SemaphoreType.DMA((3,)),
             pltpu.VMEM((ndev, msg_rows, LANES), F32),
-            pltpu.VMEM((rank, LANES), F32),
+            pltpu.VMEM((2, rank, LANES), F32),
         ],
         compiler_params=params,
         name="channel_sums",
@@ -366,8 +367,8 @@
         chan_ref[...] = new_chan
         if ndev > rank:
             out[...] = jnp.zeros_like(out)
-        channel_sums(new_chan.astype(BF16), held_spans, (buf0, buf1, buf2), None, out)
-        gs[...] = split_rows(dot(new_chan, new_chan, ((1,), (1,)), HIGHEST), rank)
+        channel_sums(new_chan.astype(BF16), held_spans, (buf0, buf1, buf2), [None] * 3, out)
+        gs[...] = split_gram(new_chan, HIGHEST)
         side = packed_side(gs, q * 8, 4)
         out[:, freq_row:, :] = jnp.zeros((ndev, msg_rows - rows, LANES), F32)
         out[:, b_row : b_row + 4, :] = jnp.broadcast_to(side[None], (ndev, 4, LANES))

time: 74.6 us -> 73.7 us (0.988)
  Pallas kernels: 22 us -> 17.1 us
  waiting for transfers between devices: 12.2 us -> 16.2 us
    pallas_call x1, Pallas kernels: 5.4 us -> 2.68 us  [body(): pl.pallas_call(hold_kernel, out_shape=(pieces[0], pieces[1], square), in_...]
    all_to_all x1, waiting for transfers between devices: 6.29 us -> 9.01 us  [body(): received = lax.all_to_all(message, ALL, 0, 0, tiled=True)]
    pallas_call x1, Pallas kernels: 3.98 us -> 2.63 us  [inverse_of(): pl.pallas_call(inverse_kernel, out_shape=jax.ShapeDtypeStruct(gram.shape,...]
    all_to_all x1, waiting for transfers between devices: 3.09 us -> 4.44 us  [body(): terms = lax.all_to_all(terms, ALL, 0, 0, tiled=True)]
    pallas_call x1, Pallas kernels: 3.68 us -> 2.86 us  [body(): pl.pallas_call(sums_kernel, out_shape=(msg, jax.ShapeDtypeStruct((SEGS, N...]
  transfers between devices with their start and end apart: 5 -> 5, of which waited for: 4 -> 4; matrix products, arithmetic and copies ran while one was open for 0% -> 0% of each run, Pallas kernels for 13% -> 7%
where the time goes in v3:
time: 73.7 us; the launch traced here: 73.5 us
  blocking collectives  32.4 us (44%)
  Pallas kernels  17.1 us (23%)
  waiting for transfers between devices  16.2 us (22%)
  starting transfers between devices  7.06 us (10%)
    all_to_all x2, blocking collectives, body(): received = lax.all_to_all(message, ALL, 0, 0, tiled=True)  32.4 us
    all_to_all x1, waiting for transfers between devices, body(): received = lax.all_to_all(message, ALL, 0, 0, tiled=True)  9.01 us
    all_to_all x1, waiting for transfers between devices, body(): terms = lax.all_to_all(terms, ALL, 0, 0, tiled=True)  4.44 us
    pallas_call x1, Pallas kernels, body(): pl.pallas_call(sums_kernel, out_shape=(msg, jax.ShapeDtypeStruct((SEGS, N...  2.86 us
    ppermute x3, waiting for transfers between devices, body(): lax.ppermute(part, 'freq', [(i, i ^ m) for i in range(nq)])  2.78 us
    pallas_call x1, Pallas kernels, body(): pl.pallas_call(hold_kernel, out_shape=(pieces[0], pieces[1], square), in_...  2.68 us
    pallas_call x1, Pallas kernels, body(): pl.pallas_call(weight_kernel, out_shape=(msg, jax.ShapeDtypeStruct((SEGS,...  2.65 us
    pallas_call x1, Pallas kernels, inverse_of(): pl.pallas_call(inverse_kernel, out_shape=jax.ShapeDtypeStruct(gram.shape,...  2.63 us
  transfers between devices with their start and end apart: 5, of which 4 were waited for; matrix products, arithmetic and copies ran while one was open for 0% of the time, Pallas kernels for 7%

profile of v3, /device:TPU:0, one launch (start us, length us, event | category | flops | bytes accessed | tf_op | source)
XLA Modules:
  0.0 73.5 jit_solution(3537055240671725512)
XLA Ops:
  0.6 0.0 copy-start
  0.6 0.0 copy-start.2
  0.7 2.9 %channel_sums.1 = (bf16[32,40,128]{2,1,0:T(8,128)(2,1)S(1)}, f32[32,1024]{1,0:T(8,128)S(1)}) custom-call(bf16[512,16896]{1,0:T(8,128)(2,1)} %signal_ref.5, bf16[32,512]{1,0:T(8,128)(2,1)} %bitcast.4, bf16[32,128]{1,0:T(8,128)(2,1)} %bitcast.6, s32[32]{0:T(128)} %win_hbm.1), custom_call_target="tpu_custom_call" | custom-call | tf_op jit(solution)/shard_map/channel_sums/pallas_call | solution.py:202
  3.5 18.8 %all_to_all.20.rcv_ref = bf16[32,40,128]{2,1,0:T(8,128)(2,1)S(1)} all-to-all(bf16[32,40,128]{2,1,0:T(8,128)(2,1)S(1)} %get-tuple-element.17), channel_id=1, replica_groups=mesh['row'=2,'col'=4,'freq'=4] {'row','col','freq'}, dimensions={0} | all-to-all | bytes 655360 | tf_op jit(solution)/shard_map/all_to_all | solution.py:240
  22.3 0.0 copy-done
  22.3 0.0 copy-done.2
  22.3 2.7 %weighting.1 = (bf16[32,40,128]{2,1,0:T(8,128)(2,1)}, f32[32,1024]{1,0:T(8,128)S(1)}, f32[32,32]{1,0:T(8,128)S(1)}, f32[32,32]{1,0:T(8,128)S(1)}) custom-call(bf16[32,40,128]{2,1,0:T(8,128)(2,1)S(1)} %all_to_all.20.rcv_ref, s32[32]{0:T(128)S(1)} %copy-done.2, f32[32,1024]{1,0:T(8,128)S(1)} %get-tuple-element.18.taper_ref, bf16[512,1024]{1,0:T(8,128)(2,1)S(1)} %copy-done), custom_call_target="tpu_custom_call" | custom-call | tf_op jit(solution)/shard_map/weighting/pallas_call | solution.py:307
  25.0 2.6 %all-to-all-start.1 = ((bf16[32,40,128]{2,1,0:T(8,128)(2,1)}), bf16[32,40,128]{2,1,0:T(8,128)(2,1)S(1)}, u32[]{:S(2)}, u32[]{:S(2)}) async-start(bf16[32,40,128]{2,1,0:T(8,128)(2,1)} %get-tuple-element.22), calls=%async_computation.1 | async-start | bytes 655360 | tf_op jit(solution)/shard_map/all_to_all | solution.py:321
  27.6 2.7 %hold_signal.1 = (bf16[512,1408]{1,0:T(8,128)(2,1)S(1)}, bf16[512,1408]{1,0:T(8,128)(2,1)S(1)}, f32[32,32]{1,0:T(8,128)S(1)}) custom-call(bf16[512,16896]{1,0:T(8,128)(2,1)} %signal_ref.5, f32[32,32]{1,0:T(8,128)S(1)} %get-tuple-element.19.gram_ref), custom_call_target="tpu_custom_call" | custom-call | tf_op jit(solution)/shard_map/hold_signal/pallas_call | solution.py:323
  30.3 9.0 %all-to-all-done.1.rcv_ref = bf16[32,40,128]{2,1,0:T(8,128)(2,1)S(1)} async-done(((bf16[32,40,128]{2,1,0:T(8,128)(2,1)}), bf16[32,40,128]{2,1,0:T(8,128)(2,1)S(1)}, u32[]{:S(2)}, u32[]{:S(2)}) %all-to-all-start.1) | async-done | bytes 327712 | tf_op jit(solution)/shard_map/all_to_all | solution.py:321
  39.3 2.6 %contraction.1 = (bf16[32,512]{1,0:T(8,128)(2,1)S(1)}, bf16[512,1408]{1,0:T(8,128)(2,1)S(1)}) custom-call(bf16[512,16896]{1,0:T(8,128)(2,1)} %signal_ref.5, bf16[512,1408]{1,0:T(8,128)(2,1)S(1)} %get-tuple-element.20.buf0, bf16[512,1408]{1,0:T(8,128)(2,1)S(1)} %get-tuple-element.21.buf1, bf16[32,40,128]{2,1,0:T(8,128)(2,1)S(1)} %all-to-all-done.1.rcv_ref, ...), custom_call_target="tpu_custom_call" | custom-call | tf_op jit(solution)/shard_map/contraction/pallas_call | solution.py:347
  41.9 0.6 collective-permute-start.2
  42.5 1.1 %collective-permute-start.1 = (bf16[32,512]{1,0:T(8,128)(2,1)S(1)}, bf16[32,512]{1,0:T(8,128)(2,1)S(1)}, u32[]{:S(2)}, u32[]{:S(2)}) collective-permute-start(bf16[32,512]{1,0:T(8,128)(2,1)S(1)} %get-tuple-element.25.p0), channel_id=1, source_target_pairs={{0,2},{1,3},{2,0},{3,1},{4,6},{5,7},{6,4},{7,5},{8,10},{9,11},{10,... | collective-permute-start | bytes 98312 | tf_op jit(solution)/shard_map/ppermute | solution.py:360
  43.5 0.3 collective-permute-start
  43.8 1.7 %collective-permute-done.2.p3 = bf16[32,512]{1,0:T(8,128)(2,1)S(1)} collective-permute-done((bf16[32,512]{1,0:T(8,128)(2,1)S(1)}, bf16[32,512]{1,0:T(8,128)(2,1)S(1)}, u32[]{:S(2)}, u32[]{:S(2)}) %collective-permute-start.2) | collective-permute-done | bytes 32800 | tf_op jit(solution)/shard_map/ppermute | solution.py:360
  45.5 1.1 %collective-permute-done.1.p2 = bf16[32,512]{1,0:T(8,128)(2,1)S(1)} collective-permute-done((bf16[32,512]{1,0:T(8,128)(2,1)S(1)}, bf16[32,512]{1,0:T(8,128)(2,1)S(1)}, u32[]{:S(2)}, u32[]{:S(2)}) %collective-permute-start.1) | collective-permute-done | bytes 32800 | tf_op jit(solution)/shard_map/ppermute | solution.py:360
  46.6 0.0 collective-permute-done.p1
  46.6 0.0 copy-start.1
  46.6 1.1 %image_sums.1 = (f32[32,512]{1,0:T(8,128)}, bf16[32,40,128]{2,1,0:T(8,128)(2,1)S(1)}) custom-call(bf16[512,1408]{1,0:T(8,128)(2,1)S(1)} %get-tuple-element.20.buf0, bf16[512,1408]{1,0:T(8,128)(2,1)S(1)} %get-tuple-element.21.buf1, bf16[512,1408]{1,0:T(8,128)(2,1)S(1)} %get-tuple-element.24.buf2, bf16[32,512]{1,0:T(8,128)(2,1)S(1)} %get-tuple-element.25.p0, ...), custom_call_target="tpu_custom_call" | custom-call | tf_op jit(solution)/shard_map/image_sums/pallas_call | solution.py:377
  47.7 13.6 %all_to_all.21.rcv_ref = bf16[32,40,128]{2,1,0:T(8,128)(2,1)S(1)} all-to-all(bf16[32,40,128]{2,1,0:T(8,128)(2,1)S(1)} %get-tuple-element.27), channel_id=1, replica_groups=mesh['row'=2,'col'=4,'freq'=4] {'row','col','freq'}, dimensions={0} | all-to-all | bytes 655360 | tf_op jit(solution)/shard_map/all_to_all | solution.py:386
  61.3 0.0 copy-done.1
  61.3 1.8 %frequency_terms.1 = (f32[32,1,128]{2,1,0:T(1,128)}, f32[32,32]{1,0:T(8,128)S(1)}) custom-call(bf16[32,40,128]{2,1,0:T(8,128)(2,1)S(1)} %all_to_all.21.rcv_ref, s32[32]{0:T(128)S(1)} %copy-done.2, f32[32,1024]{1,0:T(8,128)S(1)} %get-tuple-element.18.taper_ref, bf16[512,1024]{1,0:T(8,128)(2,1)S(1)} %copy-done.1, f32[32,1024]{1,0:T(8,128)S(1)} %get-tuple-element.28.summed_ref, ...), custom_call_target="tpu_custom_call" | custom-call | tf_op jit(solution)/shard_map/frequency_terms/pallas_call | solution.py:401
  63.1 2.5 %all-to-all-start.3 = ((f32[32,1,128]{2,1,0:T(1,128)}), f32[32,1,128]{2,1,0:T(1,128)S(1)}, u32[]{:S(2)}, u32[]{:S(2)}) async-start(f32[32,1,128]{2,1,0:T(1,128)} %get-tuple-element.30), calls=%async_computation.3 | async-start | bytes 32768 | tf_op jit(solution)/shard_map/all_to_all | solution.py:414
  65.6 2.6 %inverse.1.inverse_ref = f32[32,32]{1,0:T(8,128)S(1)} custom-call(f32[32,32]{1,0:T(8,128)S(1)} %get-tuple-element.31.gram_ref), custom_call_target="tpu_custom_call" | custom-call | tf_op jit(solution)/shard_map/inverse/pallas_call | solution.py:231
  68.3 4.4 %all-to-all-done.3.terms_ref = f32[32,1,128]{2,1,0:T(1,128)S(1)} async-done(((f32[32,1,128]{2,1,0:T(1,128)}), f32[32,1,128]{2,1,0:T(1,128)S(1)}, u32[]{:S(2)}, u32[]{:S(2)}) %all-to-all-start.3) | async-done | bytes 16416 | tf_op jit(solution)/shard_map/all_to_all | solution.py:414
  72.7 0.8 %frequency_solve.1 = f32[32,128]{1,0:T(8,128)} custom-call(f32[32,1,128]{2,1,0:T(1,128)S(1)} %all-to-all-done.3.terms_ref, f32[32,32]{1,0:T(8,128)S(1)} %inverse.1.inverse_ref), custom_call_target="tpu_custom_call" | custom-call | tf_op jit(solution)/shard_map/frequency_solve/pallas_call | solution.py:421
Async XLA Ops:
  0.6 21.7 %copy-start = (bf16[512,1024]{1,0:T(8,128)(2,1)S(1)}, bf16[512,1024]{1,0:T(8,128)(2,1)}, u32[]{:S(2)}) copy-start(bf16[512,1024]{1,0:T(8,128)(2,1)} %constant.3.table_ref) | copy-start | bytes 3145732
  0.6 21.7 %copy-start.2 = (s32[32]{0:T(128)S(1)}, s32[32]{0:T(128)}, u32[]{:S(2)}) copy-start(s32[32]{0:T(128)} %starts_ref.3) | copy-start | bytes 388
  25.0 14.3 %all-to-all-start.1 = ((bf16[32,40,128]{2,1,0:T(8,128)(2,1)}), bf16[32,40,128]{2,1,0:T(8,128)(2,1)S(1)}, u32[]{:S(2)}, u32[]{:S(2)}) async-start(bf16[32,40,128]{2,1,0:T(8,128)(2,1)} %get-tuple-element.22), calls=%async_computation.1 | async-start | bytes 655360 | tf_op jit(solution)/shard_map/all_to_all | solution.py:321
  41.9 3.6 %collective-permute-start.2 = (bf16[32,512]{1,0:T(8,128)(2,1)S(1)}, bf16[32,512]{1,0:T(8,128)(2,1)S(1)}, u32[]{:S(2)}, u32[]{:S(2)}) collective-permute-start(bf16[32,512]{1,0:T(8,128)(2,1)S(1)} %get-tuple-element.25.p0), channel_id=1, source_target_pairs={{0,3},{1,2},{2,1},{3,0},{4,7},{5,6},{6,5},{7,4},{8,11},{9,10},{10,... | collective-permute-start | bytes 98312 | tf_op jit(solution)/shard_map/ppermute | solution.py:360
  42.5 4.1 %collective-permute-start.1 = (bf16[32,512]{1,0:T(8,128)(2,1)S(1)}, bf16[32,512]{1,0:T(8,128)(2,1)S(1)}, u32[]{:S(2)}, u32[]{:S(2)}) collective-permute-start(bf16[32,512]{1,0:T(8,128)(2,1)S(1)} %get-tuple-element.25.p0), channel_id=1, source_target_pairs={{0,2},{1,3},{2,0},{3,1},{4,6},{5,7},{6,4},{7,5},{8,10},{9,11},{10,... | collective-permute-start | bytes 98312 | tf_op jit(solution)/shard_map/ppermute | solution.py:360
  43.5 3.1 %collective-permute-start = (bf16[32,512]{1,0:T(8,128)(2,1)S(1)}, bf16[32,512]{1,0:T(8,128)(2,1)S(1)}, u32[]{:S(2)}, u32[]{:S(2)}) collective-permute-start(bf16[32,512]{1,0:T(8,128)(2,1)S(1)} %get-tuple-element.25.p0), channel_id=1, source_target_pairs={{0,1},{1,0},{2,3},{3,2},{4,5},{5,4},{6,7},{7,6},{8,9},{9,8},{10,11... | collective-permute-start | bytes 98312 | tf_op jit(solution)/shard_map/ppermute | solution.py:360
  46.6 14.7 %copy-start.1 = (bf16[512,1024]{1,0:T(8,128)(2,1)S(1)}, bf16[512,1024]{1,0:T(8,128)(2,1)}, u32[]{:S(2)}) copy-start(bf16[512,1024]{1,0:T(8,128)(2,1)} %constant.3.table_ref) | copy-start | bytes 3145732
  63.1 9.6 %all-to-all-start.3 = ((f32[32,1,128]{2,1,0:T(1,128)}), f32[32,1,128]{2,1,0:T(1,128)S(1)}, u32[]{:S(2)}, u32[]{:S(2)}) async-start(f32[32,1,128]{2,1,0:T(1,128)} %get-tuple-element.30), calls=%async_computation.3 | async-start | bytes 32768 | tf_op jit(solution)/shard_map/all_to_all | solution.py:414

commit v4 on v3

v4 whole, which is shorter than its diff:
```python
import jax
import jax.numpy as jnp
import numpy as np
from jax import lax
from jax.experimental import pallas as pl
from jax.experimental.pallas import tpu as pltpu
from jax.sharding import PartitionSpec as P

NW = 1024
HALF = NW // 2
SEGS = 32
LANES = 128
ALL = ("row", "col", "freq")
F32 = jnp.float32
BF16 = jnp.bfloat16
HIGHEST = lax.Precision.HIGHEST
VMEM_BYTES = 32 << 20
AHEAD = 8
WIDE = NW + LANES
WINDOWS = 3
FIRST_SEGS = 14
PIECE = 1536


def half_table():
    position = np.arange(HALF)
    phase = (np.outer(position, position) % NW) * (2.0 * np.pi / NW)
    table = np.concatenate([np.cos(phase), -np.sin(phase)], axis=1)
    return jnp.asarray(table.astype(np.float32)).astype(BF16)


def iota(shape, axis):
    return lax.broadcasted_iota(jnp.int32, shape, axis)


def dot(a, b, contract=((1,), (0,)), precision=None):
    return lax.dot_general(
        a, b, (contract, ((), ())), precision=precision, preferred_element_type=F32
    )


def spd_inverse(system):
    size = system.shape[0]
    system = jnp.concatenate([system, jnp.zeros((size, LANES - size), F32)], axis=1)
    rows, cols = iota((size, LANES), 0), iota((size, LANES), 1)
    for i in range(size):
        col = jnp.broadcast_to(system[:, i : i + 1], (size, LANES))
        pivot = 1.0 / col[i : i + 1]
        scaled = jnp.where(cols[:1] == i, pivot, system[i : i + 1] * pivot)
        cleared = jnp.where(cols == i, 0.0, system)
        system = jnp.where(rows == i, scaled, cleared - col * scaled)
    return system[:, :size]


def split_gram(factor):
    size = factor.shape[0]
    tiled = dot(factor, jnp.concatenate([factor] * 4, axis=0), ((1,), (1,)))
    high = tiled.astype(BF16).astype(F32)
    return jnp.where(iota((size, LANES), 1) // size % 2 == 0, high, tiled - high)


def join_rows(ref, group):
    value = ref[...]
    value = value + pltpu.roll(value, LANES - 32, 1)
    other = pltpu.roll(value, 64, 1)
    return jnp.where(iota(value.shape, 0) % group < group // 2, value, other)[:, :32]


def packed_side(ref, start, count):
    upper = ref[pl.ds(start, count), :]
    lower = ref[pl.ds(start + count, count), :]
    return jnp.where(iota((count, LANES), 1) < 64, upper, lower)


def window_base(start, samples):
    base = jnp.minimum(start // LANES, samples // LANES - WIDE // LANES)
    return base, start - base * LANES


def taper_of(win_ref, starts_ref, samples):
    length = jnp.zeros((SEGS, LANES), F32)
    offset = jnp.zeros((SEGS, LANES), jnp.int32)
    which = iota((SEGS, LANES), 0)
    for k in range(SEGS):
        length = jnp.where(which == k, win_ref[k].astype(F32), length)
        offset = jnp.where(which == k, window_base(starts_ref[k], samples)[1], offset)
    scale = 1.0 / jnp.sqrt(0.375 * length)
    pieces = []
    for j in range(WIDE // LANES):
        position = (iota((SEGS, LANES), 1) + j * LANES - offset).astype(F32)
        angle = jnp.pi * (position / length - 0.5)
        square = angle * angle
        value = 1.0 + square * (
            -1.0 / 2
            + square
            * (
                1.0 / 24
                + square
                * (
                    -1.0 / 720
                    + square
                    * (1.0 / 40320 + square * (-1.0 / 3628800 + square * (1.0 / 479001600)))
                )
            )
        )
        inside = (position >= 0.0) & (position < length)
        pieces.append(jnp.where(inside, value * value * scale, 0.0))
    return jnp.concatenate(pieces, axis=1)


def forward(samples, table):
    low, high = samples[:, :HALF], samples[:, HALF:NW]
    rest = samples[:, NW:]
    low = jnp.concatenate([low[:, : WIDE - NW] + rest, low[:, WIDE - NW :]], axis=1)
    both = jnp.concatenate([low + high, low - high], axis=0)
    top = both.astype(BF16)
    rest = (both - top.astype(F32)).astype(BF16)
    out = dot(jnp.concatenate([top, rest], axis=0), table)
    out = out[: 2 * SEGS] + out[2 * SEGS :]
    return jnp.where(iota((SEGS, NW), 1) % 2 == 0, out[:SEGS], out[SEGS:])


def body(signal, starts, win_len, chan_factor, freq_factor):
    mesh_size = {name: lax.axis_size(name) for name in ALL}
    nq = mesh_size["freq"]
    nc = mesh_size["row"] * mesh_size["col"]
    ndev = nq * nc
    chans, samples = signal.shape
    bins, rank = freq_factor.shape
    span = samples // nq
    rows = span // LANES
    total_rows = rows * nq
    b_row, w_row = rows + 1, rows + 5
    msg_rows = rows + 7
    pairs = 2 * SEGS
    wide_rows = WIDE // LANES
    first_spans = [(0, 12), (12, 12), (24, rows - 24)]
    assert rank == 32 and nq == 4 and bins == LANES and ndev >= rank and nc % 8 == 0
    assert span % LANES == 0 and msg_rows % 8 == 0

    vmem = pl.BlockSpec(memory_space=pltpu.VMEM)
    smem = pl.BlockSpec(memory_space=pltpu.SMEM)
    hbm = pl.BlockSpec(memory_space=pltpu.HBM)
    params = pltpu.CompilerParams(vmem_limit_bytes=VMEM_BYTES)
    table = half_table()
    pinned = [
        pltpu.with_memory_space_constraint(x, pltpu.HBM)
        for x in (signal, chan_factor.T, freq_factor.T, win_len, starts)
    ]
    msg = jax.ShapeDtypeStruct((ndev, msg_rows, LANES), BF16)
    square = jax.ShapeDtypeStruct((rank, rank), F32)

    def fetch(signal_ref, spans, bufs, sem, ahead=8):
        base = lax.axis_index("freq") * span
        copies = []
        for i, ((first, count), buf) in enumerate(zip(spans, bufs)):
            where = pl.multiple_of(base + first * LANES, LANES)
            source = signal_ref.at[:, pl.ds(where, count * LANES)]
            copies.append(pltpu.make_async_copy(source, buf, sem.at[i]))
        for copy in copies[:ahead]:
            copy.start()
        return copies

    def channel_sums(lhs, spans, bufs, copies, out_ref, ahead=8):
        for i, (first, count) in enumerate(spans):
            if copies[i] is not None:
                copies[i].wait()
                if i + ahead < len(copies):
                    copies[i + ahead].start()
            part = dot(lhs, bufs[i][...])
            for j in range(count):
                out_ref[:rank, first + j, :] = part[:, j * LANES : (j + 1) * LANES]

    def sums_kernel(
        signal_ref, chan_hbm, freq_hbm, win_hbm, starts_hbm, msg_ref, taper_ref,
        buf, sem, chan_ref, freq_ref, win_ref, starts_ref, small, out, gs,
    ):
        small_copies = [
            pltpu.make_async_copy(chan_hbm, chan_ref, small.at[0]),
            pltpu.make_async_copy(freq_hbm, freq_ref, small.at[1]),
            pltpu.make_async_copy(win_hbm, win_ref, small.at[2]),
            pltpu.make_async_copy(starts_hbm, starts_ref, small.at[3]),
        ]
        for copy in small_copies:
            copy.start()
        bufs = [buf.at[:, a * LANES : (a + n) * LANES] for a, n in first_spans]
        copies = fetch(signal_ref, first_spans, bufs, sem, AHEAD)
        q = lax.axis_index("freq")
        c = lax.axis_index("row") * mesh_size["col"] + lax.axis_index("col")
        if ndev > rank:
            out[...] = jnp.zeros_like(out)
        for copy in small_copies:
            copy.wait()
        taper_ref[...] = taper_of(win_ref, starts_ref, samples)
        chan_low = chan_ref[...]
        weights_low = freq_ref[...]
        out[:, rows, :] = jnp.zeros((ndev, LANES), F32)
        gs[0] = split_gram(chan_low)
        gs[1] = split_gram(weights_low)
        channel_sums(chan_low, first_spans, bufs, copies, out, AHEAD)
        side = packed_side(gs.at[0], q * 8, 4)
        out[:, b_row : b_row + 4, :] = jnp.broadcast_to(side[None], (ndev, 4, LANES))
        side = packed_side(gs.at[1], (c % 8) * 4, 2)
        out[:, w_row : w_row + 2, :] = jnp.broadcast_to(side[None], (ndev, 2, LANES))
        msg_ref[...] = out[...].astype(BF16)

    message, taper = pl.pallas_call(
        sums_kernel,
        out_shape=(msg, jax.ShapeDtypeStruct((SEGS, WIDE), F32)),
        in_specs=[hbm] * 5,
        out_specs=(vmem, vmem),
        scratch_shapes=[
            pltpu.VMEM((chans, span), BF16),
            pltpu.SemaphoreType.DMA((len(first_spans),)),
            pltpu.VMEM((rank, chans), BF16),
            pltpu.VMEM((rank, bins), BF16),
            pltpu.SMEM((SEGS,), jnp.int32),
            pltpu.SMEM((SEGS,), jnp.int32),
            pltpu.SemaphoreType.DMA((4,)),
            pltpu.VMEM((ndev, msg_rows, LANES), F32),
            pltpu.VMEM((2, rank, LANES), F32),
        ],
        compiler_params=params,
        name="channel_sums",
    )(*pinned)
    received = lax.all_to_all(message, ALL, 0, 0, tiled=True)

    def spectra_part(first, count, taper, system=None):
        width = 2 * bins

        extra = () if system is None else (system,)

        def kernel(signal_ref, starts_ref, taper_ref, table_ref, *rest):
            *system_ref, spec_ref = rest[: len(extra) + 1]
            *inverse_ref, win, in_sem, out, out_sem, local = rest[len(extra) + 1 :]
            q = lax.axis_index("freq")

            def window(k, slot, side):
                where, _ = window_base(starts_ref[first + k], samples)
                where = pl.multiple_of(where * LANES, LANES)
                return pltpu.make_async_copy(
                    signal_ref.at[:, pl.ds(where, WIDE)],
                    win.at[slot, side],
                    in_sem.at[slot, side],
                )

            def store(k, side):
                where = pl.multiple_of(k * width, LANES)
                return pltpu.make_async_copy(
                    out.at[side], spec_ref.at[:, pl.ds(where, width)], out_sem.at[side]
                )

            for k in range(WINDOWS):
                for side in range(2):
                    window(2 * k + side, k, side).start()
            sign = 1 - 2 * (iota((HALF, bins), 1) % 2)
            for z in range(2):
                columns = pl.ds(pl.multiple_of(z * HALF + q * bins, LANES), bins)
                part = table_ref[:, columns]
                lanes = slice(z * bins, (z + 1) * bins)
                local[:HALF, lanes] = part
                local[HALF:NW, lanes] = (part.astype(F32) * sign.astype(F32)).astype(BF16)
                local[NW:, lanes] = part[: WIDE - NW]
            if extra:
                inverse_ref[0][...] = spd_inverse(system_ref[0][...])

            def step(k, carry):
                slot = lax.rem(k, WINDOWS)
                segments = []
                for side in range(2):
                    window(2 * k + side, slot, side).wait()
                    taper_row = taper_ref[pl.ds(first + 2 * k + side, 1), :].astype(BF16)
                    segments.append(win[slot, side] * taper_row)
                product = dot(jnp.concatenate(segments, axis=0), local[...]).astype(BF16)
                for side in range(2):

                    @pl.when(k >= 1)
                    def _():
                        store(2 * k - 2 + side, side).wait()

                    out[side] = product[side * chans : (side + 1) * chans]
                    store(2 * k + side, side).start()

                @pl.when(k + WINDOWS < count // 2)
                def _():
                    for side in range(2):
                        window(2 * (k + WINDOWS) + side, slot, side).start()

                return carry

            lax.fori_loop(0, count // 2, step, 0)
            for side in range(2):
                store(count - 2 + side, side).wait()

        spectra, *inverse = pl.pallas_call(
            kernel,
            out_shape=(pltpu.HBM((chans, count * width), BF16),) + (square,) * len(extra),
            in_specs=[hbm, smem, vmem, vmem] + [vmem] * len(extra),
            out_specs=(hbm,) + (vmem,) * len(extra),
            scratch_shapes=[
                pltpu.VMEM((WINDOWS, 2, chans, WIDE), BF16),
                pltpu.SemaphoreType.DMA((WINDOWS, 2)),
                pltpu.VMEM((2, chans, width), BF16),
                pltpu.SemaphoreType.DMA((2,)),
                pltpu.VMEM((WIDE, width), BF16),
            ],
            compiler_params=params,
            name="spectra",
        )(pinned[0], starts, taper, table, *extra)
        return [pltpu.with_memory_space_constraint(spectra, pltpu.HBM)] + inverse

    (spectra0,) = spectra_part(0, FIRST_SEGS, taper)

    def summed_kernel(
        rcv_ref, starts_ref, taper_ref, table_ref, _,
        msg_ref, system_ref, gram_ref, z_ref, y_ref, gs, out,
    ):
        for q in range(nq):
            total = rcv_ref[q].astype(F32)
            for c in range(1, nc):
                total = total + rcv_ref[c * nq + q].astype(F32)
            z_ref[q * rows : (q + 1) * rows, :] = total[:rows]
            gs[8 * q : 8 * q + 4, :] = total[b_row : b_row + 4]
            gs[8 * q + 4 : 8 * q + 8, :] = total[b_row : b_row + 4]
        gram_b = join_rows(gs, 8)
        gram_ref[...] = gram_b
        for c in range(8):
            side = rcv_ref[c * nq].astype(F32)[w_row : w_row + 2]
            for q in range(1, nq):
                side = side + rcv_ref[c * nq + q].astype(F32)[w_row : w_row + 2]
            gs[4 * c : 4 * c + 2, :] = side
            gs[4 * c + 2 : 4 * c + 4, :] = side
        system_ref[...] = gram_b * join_rows(gs, 4)
        for k in range(SEGS):
            base, _ = window_base(starts_ref[k], samples)
            y_ref[k, :wide_rows, :] = z_ref[pl.ds(base, wide_rows), :]
        windows = jnp.concatenate([y_ref[:, j, :] for j in range(wide_rows)], axis=1)
        summed = forward(windows * taper_ref[...], table_ref[...])
        for q in range(nq):
            for z in range(2):
                lanes = slice(z * HALF + q * bins, z * HALF + (q + 1) * bins)
                out[:, z, :] = summed[:, lanes]
            piece = out[...].reshape(pairs, LANES).astype(BF16)
            for c in range(nc):
                msg_ref[c * nq + q] = piece

    message, system, gram_b = pl.pallas_call(
        summed_kernel,
        out_shape=(jax.ShapeDtypeStruct((ndev, pairs, LANES), BF16), square, square),
        in_specs=[vmem, smem, vmem, vmem, hbm],
        out_specs=(vmem,) * 3,
        scratch_shapes=[
            pltpu.VMEM((total_rows, LANES), F32),
            pltpu.VMEM((SEGS, 16, LANES), F32),
            pltpu.VMEM((rank, LANES), F32),
            pltpu.VMEM((SEGS, 2, LANES), F32),
        ],
        compiler_params=params,
        name="summed",
    )(received, starts, taper, table, spectra0)
    received = lax.all_to_all(message, ALL, 0, 0, tiled=True)

    spectra1, inverse = spectra_part(FIRST_SEGS, SEGS - FIRST_SEGS, taper, system)

    width = pairs * bins
    cut0 = FIRST_SEGS * 2 * bins
    pieces = []
    for source, start, stop in ((0, 0, cut0), (1, cut0, width)):
        for at in range(start, stop, PIECE):
            pieces.append((source, at - start, at, min(PIECE, stop - at)))

    def contract_kernel(
        spec0, spec1, rcv_ref, freq_ref, inverse_ref, part_ref, summed_ref, *rest
    ):
        held, (sem, out, weighted) = rest[: len(pieces)], rest[len(pieces) :]
        copies = []
        for i, (source, begin, _, size) in enumerate(pieces):
            spec = (spec0, spec1)[source].at[:, begin : begin + size]
            copies.append(pltpu.make_async_copy(spec, held[i], sem.at[i]))
            copies[i].start()
        out[...] = rcv_ref[:rank].astype(F32)
        weights = freq_ref[...].astype(F32) / SEGS
        for j in range(pairs):
            value = out[:, j, :]
            summed_ref[:, j * LANES : (j + 1) * LANES] = value
            value = value * weights
            high = value.astype(BF16)
            weighted[:rank, j * LANES : (j + 1) * LANES] = high
            weighted[rank:, j * LANES : (j + 1) * LANES] = (value - high.astype(F32)).astype(BF16)
        total = jnp.zeros((2 * rank, chans), F32)
        for i, (_, _, start, size) in enumerate(pieces):
            copies[i].wait()
            total = total + dot(weighted[:, start : start + size], held[i][...], ((1,), (1,)))
        total = total[:rank] + total[rank:]
        part_ref[...] = dot(inverse_ref[...], total, precision=HIGHEST)

    part, summed, *held = pl.pallas_call(
        contract_kernel,
        out_shape=(
            jax.ShapeDtypeStruct((rank, chans), F32),
            jax.ShapeDtypeStruct((rank, width), F32),
        )
        + tuple(jax.ShapeDtypeStruct((chans, piece[3]), BF16) for piece in pieces),
        in_specs=[hbm, hbm, vmem, vmem, vmem],
        out_specs=(vmem,) * (2 + len(pieces)),
        scratch_shapes=[
            pltpu.SemaphoreType.DMA((len(pieces),)),
            pltpu.VMEM((rank, pairs, LANES), F32),
            pltpu.VMEM((2 * rank, pairs * LANES), BF16),
        ],
        compiler_params=params,
        name="contraction",
    )(spectra0, spectra1, received, freq_factor.T, inverse)
    parts = [part] + [
        lax.ppermute(part, "freq", [(i, i ^ m) for i in range(nq)]) for m in range(1, nq)
    ]

    last_rows = rank + 8

    def images_kernel(p0, p1, p2, p3, summed_ref, *rest):
        held, (chan_ref, msg_ref) = rest[: len(pieces)], rest[len(pieces) :]
        pair = p0[...].astype(F32) + p1[...].astype(F32)
        new_chan = pair + (p2[...].astype(F32) + p3[...].astype(F32))
        chan_ref[...] = new_chan
        rounded = new_chan.astype(BF16)
        terms = jnp.zeros((rank, bins), F32)
        for i, (_, _, start, size) in enumerate(pieces):
            images = dot(rounded, held[i][...])
            for j in range(size // LANES):
                at = start + j * LANES
                terms = terms + images[:, j * LANES : (j + 1) * LANES] * summed_ref[:, at : at + LANES]
        repeated = jnp.concatenate([new_chan] * 4, axis=0)
        gram = dot(new_chan, repeated, ((1,), (1,)), HIGHEST)
        packed = jnp.zeros((8, LANES), F32)
        for m in range(4):
            packed = jnp.where(iota((8, LANES), 1) // 32 == m, gram[8 * m : 8 * m + 8], packed)
        message = jnp.concatenate([terms / SEGS, packed], axis=0)
        msg_ref[...] = jnp.broadcast_to(message[None], (nc, last_rows, LANES))

    new_chan, message = pl.pallas_call(
        images_kernel,
        out_shape=(
            jax.ShapeDtypeStruct((rank, chans), F32),
            jax.ShapeDtypeStruct((nc, last_rows, LANES), F32),
        ),
        in_specs=[vmem] * (5 + len(pieces)),
        out_specs=(vmem, vmem),
        compiler_params=params,
        name="images",
    )(*parts, summed, *held)
    received = lax.all_to_all(message, ("row", "col"), 0, 0, tiled=True)

    def finish_kernel(rcv_ref, gram_ref, out_ref):
        total = rcv_ref[0]
        for c in range(1, nc):
            total = total + rcv_ref[c]
        packed = total[rank:]
        gram_a = jnp.concatenate(
            [pltpu.roll(packed, (LANES - 32 * m) % LANES, 1)[:, :32] for m in range(4)], axis=0
        )
        inverse = spd_inverse(gram_a * gram_ref[...])
        out_ref[...] = dot(inverse, total[:rank], precision=HIGHEST)

    new_freq = pl.pallas_call(
        finish_kernel,
        out_shape=jax.ShapeDtypeStruct((rank, bins), F32),
        in_specs=[vmem, vmem],
        out_specs=vmem,
        compiler_params=params,
        name="frequency_solve",
    )(received, gram_b)
    return (new_chan.T, new_freq.T)


def solution(mesh):
    return jax.shard_map(
        body,
        mesh=mesh,
        in_specs=(P(("row", "col"), None), P(), P(), P(("row", "col"), None), P("freq", None)),
        out_specs=(P(("row", "col"), None), P("freq", None)),
        check_vma=False,
    )
```

time: 73.7 us -> 72.6 us (0.985)
  Pallas kernels: 17.1 us -> 38.5 us
  blocking collectives: 32.4 us -> 11.1 us
  waiting for transfers between devices: 16.2 us -> 8.51 us
  starting transfers between devices: 7.06 us -> 13.3 us
    all_to_all x2 -> x1, blocking collectives: 32.4 us -> 11.1 us  [body(): received = lax.all_to_all(message, ('row', 'col'), 0, 0, tiled=True)]
    pallas_call x5 -> x4, Pallas kernels: 12.6 us -> 28.5 us  [the longest x2 23 us: spectra_part(): pl.pallas_call(kernel, out_shape=(pltpu.HBM((chans, count * width), BF16)...]
    all_to_all x1 -> x2, starting transfers between devices: 2.59 us -> 11.4 us  [body(): received = lax.all_to_all(message, ALL, 0, 0, tiled=True)]
    all_to_all x1 -> x0, waiting for transfers between devices: 4.44 us -> none  [body(): terms = lax.all_to_all(terms, ALL, 0, 0, tiled=True)]
    all_to_all x1 -> x2, waiting for transfers between devices: 9.01 us -> 4.57 us  [body(): received = lax.all_to_all(message, ALL, 0, 0, tiled=True)]
    pallas_call x1, Pallas kernels: 0.76 us -> 3.41 us  [body(): pl.pallas_call(finish_kernel, out_shape=jax.ShapeDtypeStruct((rank, bins)...]
    all_to_all x1 -> x0, starting transfers between devices: 2.54 us -> none  [body(): terms = lax.all_to_all(terms, ALL, 0, 0, tiled=True)]
    pallas_call x1, Pallas kernels: 2.62 us -> 4.81 us  [body(): pl.pallas_call(contract_kernel, out_shape=(jax.ShapeDtypeStruct((rank, ch...]
  transfers between devices with their start and end apart: 5 -> 5, of which waited for: 4 -> 4; matrix products, arithmetic and copies ran while one was open for 0% -> 0% of each run, Pallas kernels for 7% -> 32%
where the time goes in v4:
time: 72.6 us; the launch traced here: 72.3 us
  Pallas kernels  38.5 us (53%)
  starting transfers between devices  13.3 us (18%)
  blocking collectives  11.1 us (15%)
  waiting for transfers between devices  8.51 us (12%)
  between operations  0.73 us (1%)
    pallas_call x2, Pallas kernels, spectra_part(): pl.pallas_call(kernel, out_shape=(pltpu.HBM((chans, count * width), BF16)...  23 us
    all_to_all x2, starting transfers between devices, body(): received = lax.all_to_all(message, ALL, 0, 0, tiled=True)  11.4 us
    all_to_all x1, blocking collectives, body(): received = lax.all_to_all(message, ('row', 'col'), 0, 0, tiled=True)  11.1 us
    pallas_call x1, Pallas kernels, body(): pl.pallas_call(contract_kernel, out_shape=(jax.ShapeDtypeStruct((rank, ch...  4.81 us
    all_to_all x2, waiting for transfers between devices, body(): received = lax.all_to_all(message, ALL, 0, 0, tiled=True)  4.57 us
    ppermute x3, waiting for transfers between devices, body(): lax.ppermute(part, 'freq', [(i, i ^ m) for i in range(nq)])  3.94 us
    pallas_call x1, Pallas kernels, body(): pl.pallas_call(sums_kernel, out_shape=(msg, jax.ShapeDtypeStruct((SEGS, W...  3.58 us
    pallas_call x1, Pallas kernels, body(): pl.pallas_call(finish_kernel, out_shape=jax.ShapeDtypeStruct((rank, bins)...  3.41 us
  transfers between devices with their start and end apart: 5, of which 4 were waited for; matrix products, arithmetic and copies ran while one was open for 0% of the time, Pallas kernels for 32%

profile of v4, /device:TPU:0, one launch (start us, length us, event | category | flops | bytes accessed | tf_op | source)
XLA Modules:
  0.0 72.3 jit_solution(6997741627870685956)
XLA Ops:
  0.6 0.0 copy-start
  0.6 0.0 copy-start.2
  0.7 3.6 %channel_sums.1 = (bf16[32,40,128]{2,1,0:T(8,128)(2,1)}, f32[32,1152]{1,0:T(8,128)S(1)}) custom-call(bf16[512,16896]{1,0:T(8,128)(2,1)} %signal_ref.5, bf16[32,512]{1,0:T(8,128)(2,1)} %bitcast.6, bf16[32,128]{1,0:T(8,128)(2,1)} %bitcast.4, s32[32]{0:T(128)} %win_hbm.1, s32[32]{0:T(128)} %starts_ref.5), custom_call_target="tpu_custom_call" | custom-call | tf_op jit(solution)/shard_map/channel_sums/pallas_call | solution.py:207
  4.2 7.3 %all-to-all-start = ((bf16[32,40,128]{2,1,0:T(8,128)(2,1)}), bf16[32,40,128]{2,1,0:T(8,128)(2,1)S(1)}, u32[]{:S(2)}, u32[]{:S(2)}) async-start(bf16[32,40,128]{2,1,0:T(8,128)(2,1)} %get-tuple-element.20), calls=%async_computation | async-start | bytes 655360 | tf_op jit(solution)/shard_map/all_to_all | solution.py:226
  11.5 0.0 copy-done
  11.6 0.0 copy-done.2
  11.6 9.9 %spectra.2._.spec0 = bf16[512,3584]{1,0:T(8,128)(2,1)} custom-call(bf16[512,16896]{1,0:T(8,128)(2,1)} %signal_ref.5, s32[32]{0:T(128)S(1)} %copy-done.2, f32[32,1152]{1,0:T(8,128)S(1)} %get-tuple-element.19.taper_ref, bf16[512,1024]{1,0:T(8,128)(2,1)S(1)} %copy-done), custom_call_target="tpu_custom_call" | custom-call | tf_op jit(solution)/shard_map/spectra/pallas_call | solution.py:295
  21.5 1.7 %all-to-all-done.rcv_ref = bf16[32,40,128]{2,1,0:T(8,128)(2,1)S(1)} async-done(((bf16[32,40,128]{2,1,0:T(8,128)(2,1)}), bf16[32,40,128]{2,1,0:T(8,128)(2,1)S(1)}, u32[]{:S(2)}, u32[]{:S(2)}) %all-to-all-start) | async-done | bytes 327712 | tf_op jit(solution)/shard_map/all_to_all | solution.py:226
  23.2 2.0 %summed.1 = (bf16[32,64,128]{2,1,0:T(8,128)(2,1)}, f32[32,32]{1,0:T(8,128)S(1)}, f32[32,32]{1,0:T(8,128)S(1)}) custom-call(bf16[32,40,128]{2,1,0:T(8,128)(2,1)S(1)} %all-to-all-done.rcv_ref, s32[32]{0:T(128)S(1)} %copy-done.2, f32[32,1152]{1,0:T(8,128)S(1)} %get-tuple-element.19.taper_ref, bf16[512,1024]{1,0:T(8,128)(2,1)S(1)} %copy-done, ...), custom_call_target="tpu_custom_call" | custom-call | tf_op jit(solution)/shard_map/summed/pallas_call | solution.py:347
  25.2 4.1 %all-to-all-start.1 = ((bf16[32,64,128]{2,1,0:T(8,128)(2,1)}), bf16[32,64,128]{2,1,0:T(8,128)(2,1)S(1)}, u32[]{:S(2)}, u32[]{:S(2)}) async-start(bf16[32,64,128]{2,1,0:T(8,128)(2,1)} %get-tuple-element.23), calls=%async_computation.1 | async-start | bytes 1048576 | tf_op jit(solution)/shard_map/all_to_all | solution.py:361
  29.3 0.0 copy-start.1
  29.4 13.1 %spectra.3 = (bf16[512,4608]{1,0:T(8,128)(2,1)}, f32[32,32]{1,0:T(8,128)S(1)}) custom-call(bf16[512,16896]{1,0:T(8,128)(2,1)} %signal_ref.5, s32[32]{0:T(128)S(1)} %copy-done.2, f32[32,1152]{1,0:T(8,128)S(1)} %get-tuple-element.19.taper_ref, bf16[512,1024]{1,0:T(8,128)(2,1)S(1)} %copy-done, f32[32,32]{1,0:T(8,128)S(1)} %get-tuple-element.21.rest_0_), custom_call_target="tpu_custom_call" | custom-call | tf_op jit(solution)/shard_map/spectra/pallas_call | solution.py:295
  42.4 2.8 %all-to-all-done.1.rcv_ref = bf16[32,64,128]{2,1,0:T(8,128)(2,1)S(1)} async-done(((bf16[32,64,128]{2,1,0:T(8,128)(2,1)}), bf16[32,64,128]{2,1,0:T(8,128)(2,1)S(1)}, u32[]{:S(2)}, u32[]{:S(2)}) %all-to-all-start.1) | async-done | bytes 524320 | tf_op jit(solution)/shard_map/all_to_all | solution.py:361
  45.3 0.0 copy-done.1
  45.3 4.8 %contraction.1 = (f32[32,512]{1,0:T(8,128)S(1)}, f32[32,8192]{1,0:T(8,128)S(1)}, bf16[512,1536]{1,0:T(8,128)(2,1)S(1)}, bf16[512,1536]{1,0:T(8,128)(2,1)S(1)}, b...) custom-call(bf16[512,3584]{1,0:T(8,128)(2,1)} %spectra.2._.spec0, ...), custom_call_target="tpu_custom_call" | custom-call | tf_op jit(solution)/shard_map/contraction/pallas_call | solution.py:397
  50.1 0.3 collective-permute-start.2
  50.4 1.3 %collective-permute-start.1 = (f32[32,512]{1,0:T(8,128)S(1)}, f32[32,512]{1,0:T(8,128)S(1)}, u32[]{:S(2)}, u32[]{:S(2)}) collective-permute-start(f32[32,512]{1,0:T(8,128)S(1)} %get-tuple-element.25.p0), channel_id=1, source_target_pairs={{0,2},{1,3},{2,0},{3,1},{4,6},{5,7},{6,4},{7,5},{8,10},{9,11},{10,... | collective-permute-start | bytes 196616 | tf_op jit(solution)/shard_map/ppermute | solution.py:415
  51.7 0.3 collective-permute-start
  52.0 2.5 %collective-permute-done.2.p3 = f32[32,512]{1,0:T(8,128)S(1)} collective-permute-done((f32[32,512]{1,0:T(8,128)S(1)}, f32[32,512]{1,0:T(8,128)S(1)}, u32[]{:S(2)}, u32[]{:S(2)}) %collective-permute-start.2) | collective-permute-done | bytes 65568 | tf_op jit(solution)/shard_map/ppermute | solution.py:415
  54.5 1.4 %collective-permute-done.1.p2 = f32[32,512]{1,0:T(8,128)S(1)} collective-permute-done((f32[32,512]{1,0:T(8,128)S(1)}, f32[32,512]{1,0:T(8,128)S(1)}, u32[]{:S(2)}, u32[]{:S(2)}) %collective-permute-start.1) | collective-permute-done | bytes 65568 | tf_op jit(solution)/shard_map/ppermute | solution.py:415
  55.9 0.0 collective-permute-done.p1
  55.9 1.8 %images.1 = (f32[32,512]{1,0:T(8,128)}, f32[8,40,128]{2,1,0:T(8,128)S(1)}) custom-call(f32[32,512]{1,0:T(8,128)S(1)} %get-tuple-element.25.p0, f32[32,512]{1,0:T(8,128)S(1)} %collective-permute-done.p1, f32[32,512]{1,0:T(8,128)S(1)} %collective-permute-done.1.p2, f32[32,512]{1,0:T(8,128)S(1)} %collective-permute-done.2.p3, ...), custom_call_target="tpu_custom_call" | custom-call | tf_op jit(solution)/shard_map/images/pallas_call | solution.py:440
  57.7 11.1 %all_to_all.15.rcv_ref = f32[8,40,128]{2,1,0:T(8,128)S(1)} all-to-all(f32[8,40,128]{2,1,0:T(8,128)S(1)} %get-tuple-element.34), channel_id=1, replica_groups=mesh['row'=2,'col'=4,'freq'=4] {'row','col'}, dimensions={0} | all-to-all | bytes 327680 | tf_op jit(solution)/shard_map/all_to_all | solution.py:451
  68.8 3.4 %frequency_solve.1 = f32[32,128]{1,0:T(8,128)} custom-call(f32[8,40,128]{2,1,0:T(8,128)S(1)} %all_to_all.15.rcv_ref, f32[32,32]{1,0:T(8,128)S(1)} %get-tuple-element.35.gram_ref), custom_call_target="tpu_custom_call" | custom-call | tf_op jit(solution)/shard_map/frequency_solve/pallas_call | solution.py:464
Async XLA Ops:
  0.6 10.9 %copy-start = (bf16[512,1024]{1,0:T(8,128)(2,1)S(1)}, bf16[512,1024]{1,0:T(8,128)(2,1)}, u32[]{:S(2)}) copy-start(bf16[512,1024]{1,0:T(8,128)(2,1)} %constant.3.table_ref) | copy-start | bytes 3145732
  0.6 10.9 %copy-start.2 = (s32[32]{0:T(128)S(1)}, s32[32]{0:T(128)}, u32[]{:S(2)}) copy-start(s32[32]{0:T(128)} %starts_ref.5) | copy-start | bytes 388
  4.2 19.0 %all-to-all-start = ((bf16[32,40,128]{2,1,0:T(8,128)(2,1)}), bf16[32,40,128]{2,1,0:T(8,128)(2,1)S(1)}, u32[]{:S(2)}, u32[]{:S(2)}) async-start(bf16[32,40,128]{2,1,0:T(8,128)(2,1)} %get-tuple-element.20), calls=%async_computation | async-start | bytes 655360 | tf_op jit(solution)/shard_map/all_to_all | solution.py:226
  25.2 20.0 %all-to-all-start.1 = ((bf16[32,64,128]{2,1,0:T(8,128)(2,1)}), bf16[32,64,128]{2,1,0:T(8,128)(2,1)S(1)}, u32[]{:S(2)}, u32[]{:S(2)}) async-start(bf16[32,64,128]{2,1,0:T(8,128)(2,1)} %get-tuple-element.23), calls=%async_computation.1 | async-start | bytes 1048576 | tf_op jit(solution)/shard_map/all_to_all | solution.py:361
  29.3 15.9 %copy-start.1 = (bf16[128,32]{0,1:T(8,128)(2,1)S(1)}, bf16[128,32]{0,1:T(8,128)(2,1)}, u32[]{:S(2)}) copy-start(bf16[128,32]{0,1:T(8,128)(2,1)} %param.10) | copy-start | bytes 24580
  50.1 4.4 %collective-permute-start.2 = (f32[32,512]{1,0:T(8,128)S(1)}, f32[32,512]{1,0:T(8,128)S(1)}, u32[]{:S(2)}, u32[]{:S(2)}) collective-permute-start(f32[32,512]{1,0:T(8,128)S(1)} %get-tuple-element.25.p0), channel_id=1, source_target_pairs={{0,3},{1,2},{2,1},{3,0},{4,7},{5,6},{6,5},{7,4},{8,11},{9,10},{10,... | collective-permute-start | bytes 196616 | tf_op jit(solution)/shard_map/ppermute | solution.py:415
  50.4 5.5 %collective-permute-start.1 = (f32[32,512]{1,0:T(8,128)S(1)}, f32[32,512]{1,0:T(8,128)S(1)}, u32[]{:S(2)}, u32[]{:S(2)}) collective-permute-start(f32[32,512]{1,0:T(8,128)S(1)} %get-tuple-element.25.p0), channel_id=1, source_target_pairs={{0,2},{1,3},{2,0},{3,1},{4,6},{5,7},{6,4},{7,5},{8,10},{9,11},{10,... | collective-permute-start | bytes 196616 | tf_op jit(solution)/shard_map/ppermute | solution.py:415
  51.7 4.2 %collective-permute-start = (f32[32,512]{1,0:T(8,128)S(1)}, f32[32,512]{1,0:T(8,128)S(1)}, u32[]{:S(2)}, u32[]{:S(2)}) collective-permute-start(f32[32,512]{1,0:T(8,128)S(1)} %get-tuple-element.25.p0), channel_id=1, source_target_pairs={{0,1},{1,0},{2,3},{3,2},{4,5},{5,4},{6,7},{7,6},{8,9},{9,8},{10,11... | collective-permute-start | bytes 196616 | tf_op jit(solution)/shard_map/ppermute | solution.py:415
